TPU v7x, 256 devices: a whole 4x4x8 slice. The times are simulated.
256 devices in a mesh: segment: 2 (over core), tensor: 16 (over x, z_hi), dp: 8 (over z_lo, y).
Axes of the slice: x: 4, y: 4, z: 8 (z_hi: 4, z_lo: 2; z = z_hi * 2 + z_lo), core: 2. Of those that a mesh axis runs over, the one named last changes fastest.
Arguments:
- tokens: bfloat16 [1024, 1536], P('dp', 'tensor'), may hold values from -6 to 6
- w_gate: bfloat16 [2, 1536, 12288], P('segment', None, 'tensor'), may hold values from -0.15625 to 0.15625
- w_up: bfloat16 [2, 1536, 12288], P('segment', None, 'tensor'), may hold values from -0.15625 to 0.15625
- w_down: bfloat16 [2, 12288, 1536], P('segment', 'tensor'), may hold values from -0.0546875 to 0.0546875
- cotangent: bfloat16 [1024, 1536], P('dp', 'tensor'), may hold values from -0.1796875 to 0.1796875
Outputs:
- grad_gate: float32 [2, 1536, 12288], P('segment', 'dp', 'tensor')
- grad_up: float32 [2, 1536, 12288], P('segment', 'dp', 'tensor')
- grad_down: float32 [2, 12288, 1536], P('segment', 'tensor', 'dp')
All inputs are finite; a program needn't handle non-finite values.
Results may differ from a plain program's by a relative error of at most 0.023.
Values may be sent and summed in bfloat16 or wider, within the bound.
No kernel may reach another device: no remote copies, remote signals or barrier semaphores. Data moves between devices by JAX's collectives and lax.ppermute only.
A program may use at most 64 MiB of HBM per device.

v0:
```python
import jax
import jax.numpy as jnp
from jax import lax
from jax.experimental import pallas as pl
from jax.experimental.pallas import tpu as pltpu
from jax.sharding import Mesh, PartitionSpec as P


CORES = 2
XS = 4
ZH = 4
ZL = 2
YS = 4
PEERS = ZL * YS
LANES = 128
TENSOR = ("x", "zh")
DP = ("zl", "y")
BF16 = jnp.bfloat16
F32 = jnp.float32


def shifted(value, axis, distance):
    size = lax.axis_size(axis)
    return lax.ppermute(value, axis, [(i, (i + distance) % size) for i in range(size)])


def fanned(value_of, axis, distance_of):
    out = []
    for k in range(1, lax.axis_size(axis)):
        out.append(shifted(value_of(k), axis, distance_of(k)))
    return out


def one_way(value, source):
    return lax.ppermute(value, "segment", [(source, 1 - source)])


def exchanged(value, axes):
    return lax.all_to_all(value, axes, 0, 0, tiled=True)


def dot_tn(left, right):
    return lax.dot_general(left, right, (((0,), (0,)), ((), ())), preferred_element_type=F32)


def dot_nt(left, right):
    return lax.dot_general(left, right, (((1,), (1,)), ((), ())), preferred_element_type=F32)


def dot_nn(left, right):
    return jnp.dot(left, right, preferred_element_type=F32)


def whole(memory_space=pltpu.VMEM):
    return pl.BlockSpec(memory_space=memory_space)


def hidden_of(gate, up):
    gate = gate.astype(F32)
    return (jax.nn.silu(gate) * up.astype(F32)).astype(BF16)


def gate_grads(d_hidden, gate, up):
    gate = gate.astype(F32)
    up = up.astype(F32)
    sigma = jax.nn.sigmoid(gate)
    d_gate = (d_hidden * up * sigma * (1.0 + gate * (1.0 - sigma))).astype(BF16)
    d_up = (d_hidden * gate * sigma).astype(BF16)
    return d_gate, d_up


def limits(mebibytes):
    return pltpu.CompilerParams(vmem_limit_bytes=mebibytes * 2**20)


def columns_at(value, index, width):
    return lax.dynamic_slice_in_dim(value, index * width, width, 1)


def spread(first, second, core):
    def body(core_ref, first_ref, second_ref, out_ref):
        value = jnp.where(core_ref[0] == 0, first_ref[...], second_ref[...])
        for i in range(XS * ZH):
            out_ref[i] = value

    shape = (XS * ZH, *first.shape)
    values = [pltpu.with_memory_space_constraint(v, pltpu.HBM) for v in (first, second)]
    return pl.pallas_call(
        body,
        grid=(1,),
        in_specs=[whole(pltpu.SMEM)] + [pl.BlockSpec(first.shape, lambda i: (0, 0))] * 2,
        out_specs=pl.BlockSpec(shape, lambda i: (0, 0, 0)),
        out_shape=jax.ShapeDtypeStruct(shape, BF16),
        compiler_params=limits(2),
        name="spread",
    )(core, *values)


def assemble(blocks, x):
    rows, width = blocks[0].shape

    def body(x_ref, *refs):
        out_ref = refs[-1]
        for k in range(XS):
            start = pl.multiple_of(((x_ref[0] + k) % XS) * width, LANES)
            out_ref[:, pl.ds(start, width)] = refs[k][...]

    return pl.pallas_call(
        body,
        in_specs=[whole(pltpu.SMEM)] + [whole()] * XS,
        out_specs=whole(),
        out_shape=jax.ShapeDtypeStruct((rows, width * XS), BF16),
        compiler_params=limits(2),
        name="assemble",
    )(x, *blocks)


def merge(own, other, core):
    rows, width = own.shape

    def body(core_ref, own_ref, other_ref, out_ref):
        start = pl.multiple_of(core_ref[0] * rows, 16)
        out_ref[pl.ds(start, rows), :] = own_ref[...]
        start = pl.multiple_of((1 - core_ref[0]) * rows, 16)
        out_ref[pl.ds(start, rows), :] = other_ref[...]

    return pl.pallas_call(
        body,
        in_specs=[whole(pltpu.SMEM), whole(), whole()],
        out_specs=whole(),
        out_shape=jax.ShapeDtypeStruct((rows * CORES, width), BF16),
        compiler_params=limits(2),
        name="merge",
    )(core, own, other)


def picked(by_core, core):
    rows, width = by_core[0][0][0].shape
    half = width // CORES
    count = max(len(picks) for picks in by_core)
    values = []
    for picks in by_core:
        for value, _ in picks:
            if not any(value is known for known in values):
                values.append(value)

    def body(core_ref, *refs):
        out_ref = refs[-1]
        for c, picks in enumerate(by_core):

            @pl.when(core_ref[0] == c)
            def _(picks=picks):
                for slot in range(count):
                    value, side = picks[min(slot, len(picks) - 1)]
                    at = [value is known for known in values].index(True)
                    out_ref[slot] = refs[at][:, side * half : (side + 1) * half]

    return pl.pallas_call(
        body,
        in_specs=[whole(pltpu.SMEM)] + [whole()] * len(values),
        out_specs=whole(),
        out_shape=jax.ShapeDtypeStruct((count, rows, half), BF16),
        compiler_params=limits(4),
        name="picked",
    )(core, *values)


def packed(choices, given, acts, core, shared=False):
    rows = choices[0][0].shape[0]
    half = choices[0][0].shape[1] // (1 if given is None else CORES)
    tiles = half // LANES
    group = 4
    turned = isinstance(acts, tuple)
    features = acts[0].shape[1] if turned else acts.shape[0]
    shard = features // PEERS
    count = len(choices)
    part = shard // CORES if shared else shard
    height = count * tiles * rows + part
    values = [choice[0] for choice in choices]
    specs = [pl.BlockSpec(value.shape, lambda p: (0, 0)) for value in values]
    if given is not None:
        values.append(given)
        specs.append(pl.BlockSpec(given.shape, lambda p: (0, 0, 0)))
    if turned:
        values.append(acts[0])
        specs.append(pl.BlockSpec(acts[0].shape, lambda p: (0, 0)))
    else:
        values.append(acts)
        specs.append(pl.BlockSpec((group * shard, rows), lambda p: (p, 0)))

    def body(core_ref, *refs):
        given_ref = None if given is None else refs[count]
        out_ref = refs[len(values)]
        index = pl.program_id(0)
        for c, (_, source, slot) in enumerate(choices):
            for t in range(tiles):
                base = (c * tiles + t) * rows
                first = (source or 0) * half + t * LANES
                tile = refs[c][:, first : first + LANES]
                if source is not None:
                    other = given_ref[slot, :, t * LANES : (t + 1) * LANES]
                    tile = jnp.where(core_ref[0] == source, tile, other)
                for g in range(group):
                    out_ref[g, base : base + rows, :] = tile
        if turned:
            acts_ref = refs[len(values) - 1]
            turned_ref = refs[-1]

            @pl.when(index == 0)
            def _():
                for t in range(features // LANES):
                    at = slice(t * LANES, (t + 1) * LANES)
                    turned_ref[at, :] = acts_ref[:, at].T

            for g in range(group):
                start = (index * group + g) * shard
                if shared:
                    start = start + core_ref[0] * part
                start = pl.multiple_of(start, 32)
                out_ref[g, count * tiles * rows :, :] = turned_ref[pl.ds(start, part), :]
        else:
            acts_ref = refs[len(values) - 1]
            for g in range(group):
                at = slice(g * shard, (g + 1) * shard)
                out_ref[g, count * tiles * rows :, :] = acts_ref[at, :]

    return pl.pallas_call(
        body,
        grid=(PEERS // group,),
        in_specs=[whole(pltpu.SMEM)] + specs,
        out_specs=pl.BlockSpec((group, height, rows), lambda p: (p, 0, 0)),
        out_shape=jax.ShapeDtypeStruct((PEERS, height, rows), BF16),
        scratch_shapes=[pltpu.VMEM((features, rows), BF16)] if turned else [],
        compiler_params=limits(8),
        name="packed",
    )(core, *values)


def tiled(ref, k, base, lanes):
    return jnp.concatenate(
        [ref[k, base + t * lanes : base + (t + 1) * lanes, :] for t in range(3)], axis=1
    )


def add_grads(out_ref, low_ref, turn, turns, gate, up, grad, acts, upstream):
    gate = gate.astype(F32)
    up = up.astype(F32)
    grad = grad.astype(F32)
    sigma = jax.nn.sigmoid(gate)
    silu = gate * sigma
    d_gate = (grad * up * sigma * (1.0 + gate * (1.0 - sigma))).astype(BF16)
    parts = [
        dot_nn(acts, d_gate),
        dot_nn(acts, (grad * silu).astype(BF16)),
        dot_nn(upstream, (silu * up).astype(BF16)),
    ]
    for i, part in enumerate(parts):
        total = part if turn == 0 else out_ref[i] + part
        out_ref[i] = total
        if turn == turns - 1:
            low_ref[i] = total.astype(BF16)


def first_grads(stored, entry, entry_other, acts_other, core):
    peers, height, lanes = stored.shape
    half = 3 * lanes
    shard = entry_other.shape[1]
    tail = half + shard
    step = 2

    def body(core_ref, stored_ref, entry_ref, entry_other_ref, acts_other_ref, *refs):
        out_ref, low_ref, own_ref, late_ref, cot_ref, acts_ref, sems, whole_sems = refs
        wholes = [
            pltpu.make_async_copy(entry_other_ref, cot_ref, whole_sems.at[0]),
            pltpu.make_async_copy(acts_other_ref, acts_ref, whole_sems.at[1]),
        ]
        copies = []
        for k in range(peers):
            copies.append(
                [
                    pltpu.make_async_copy(stored_ref.at[k], own_ref.at[k], sems.at[k, 0]),
                    pltpu.make_async_copy(
                        entry_ref.at[k, pl.ds(2 * half, tail)], late_ref.at[k], sems.at[k, 1]
                    ),
                ]
            )
            for copy in copies[k]:
                copy.start()
            if k == 0:
                for copy in wholes:
                    copy.start()
        for copy in wholes:
            copy.wait()
        first = core_ref[0] == 0
        for turn in range(peers // step):
            ks = range(step * turn, step * (turn + 1))
            for k in ks:
                for copy in copies[k]:
                    copy.wait()

            def over(ref, base):
                return jnp.concatenate([tiled(ref, k, base, lanes) for k in ks], axis=0)

            acts = []
            upstream = []
            for k in ks:
                mine = own_ref[k, 2 * half :, :]
                other = acts_ref[k]
                acts.append(
                    jnp.concatenate(
                        [jnp.where(first, mine, other), jnp.where(first, other, mine)], axis=0
                    )
                )
                upstream.append(jnp.where(first, cot_ref[k], late_ref[k, half:, :]))
            add_grads(
                out_ref,
                low_ref,
                turn,
                peers // step,
                over(own_ref, 0),
                over(own_ref, half),
                over(late_ref, 0),
                jnp.concatenate(acts, axis=1),
                jnp.concatenate(upstream, axis=1),
            )

    shape = (3, shard, half)
    values = [pltpu.with_memory_space_constraint(v, pltpu.HBM) for v in (stored, entry, entry_other)]
    return pl.pallas_call(
        body,
        in_specs=[whole(pltpu.SMEM)] + [whole(pl.ANY)] * 4,
        out_specs=[whole()] * 2,
        out_shape=[jax.ShapeDtypeStruct(shape, F32), jax.ShapeDtypeStruct(shape, BF16)],
        scratch_shapes=[
            pltpu.VMEM((peers, height, lanes), BF16),
            pltpu.VMEM((peers, tail, lanes), BF16),
            pltpu.VMEM(entry_other.shape, BF16),
            pltpu.VMEM(acts_other.shape, BF16),
            pltpu.SemaphoreType.DMA((peers, 2)),
            pltpu.SemaphoreType.DMA((2,)),
        ],
        compiler_params=limits(16),
        name="first_grads",
    )(core, *values, acts_other)


def packed_late(d_hidden, upstream, place):
    rows, half = d_hidden.shape
    features = upstream.shape[1]
    shard = features // PEERS
    tiles = half // LANES

    def body(place_ref, grad_ref, up_ref, *refs):
        outs = refs[:PEERS]
        turned_ref = refs[PEERS]
        for t in range(features // LANES):
            at = slice(t * LANES, (t + 1) * LANES)
            turned_ref[at, :] = up_ref[:, at].T
        for k in range(PEERS):
            for t in range(tiles):
                outs[k][t * rows : (t + 1) * rows, :] = grad_ref[:, t * LANES : (t + 1) * LANES]
            start = pl.multiple_of(((place_ref[1] + k) % PEERS) * shard, 64)
            outs[k][tiles * rows :, :] = turned_ref[pl.ds(start, shard), :]

    shape = jax.ShapeDtypeStruct((tiles * rows + shard, rows), BF16)
    return pl.pallas_call(
        body,
        in_specs=[whole(pltpu.SMEM), whole(), whole()],
        out_specs=[whole()] * PEERS,
        out_shape=[shape] * PEERS,
        scratch_shapes=[pltpu.VMEM((features, rows), BF16)],
        compiler_params=limits(4),
        name="packed_late",
    )(place, d_hidden, upstream)


def last_grads(wide, other, late, place):
    peers, height, lanes = wide.shape
    shard = other.shape[1]
    half = 3 * lanes
    step = 2

    def body(place_ref, wide_ref, other_ref, *refs):
        late_refs = refs[:peers]
        out_ref, low_ref, stored_ref, acts_ref, swapped_ref, sems = refs[peers:]
        copies = []
        for k in range(peers):
            replica = (place_ref[1] + peers - k) % peers
            moves = [
                (wide_ref.at[replica, pl.ds(0, 2 * half)], stored_ref),
                (wide_ref.at[replica, pl.ds(height - shard, shard)], acts_ref),
                (other_ref.at[replica], swapped_ref),
            ]
            copies.append(
                [
                    pltpu.make_async_copy(source, target.at[k], sems.at[k, i])
                    for i, (source, target) in enumerate(moves)
                ]
            )
            for copy in copies[k]:
                copy.start()

        mine = place_ref[0] == 0
        for turn in range(peers // step):
            ks = range(step * turn, step * (turn + 1))
            for k in ks:
                for copy in copies[k]:
                    copy.wait()

            def over(ref, base):
                return jnp.concatenate([tiled(ref, k, base, lanes) for k in ks], axis=0)

            grad = jnp.concatenate(
                [
                    jnp.concatenate(
                        [late_refs[k][t * lanes : (t + 1) * lanes, :] for t in range(3)], axis=1
                    )
                    for k in ks
                ],
                axis=0,
            )
            add_grads(
                out_ref,
                low_ref,
                turn,
                peers // step,
                over(stored_ref, 0),
                over(stored_ref, half),
                grad,
                jnp.concatenate(
                    [jnp.where(mine, acts_ref[k], swapped_ref[k]) for k in ks], axis=1
                ),
                jnp.concatenate([late_refs[k][half:, :] for k in ks], axis=1),
            )

    shape = (3, shard, half)
    return pl.pallas_call(
        body,
        in_specs=[whole(pltpu.SMEM), whole(pl.ANY), whole(pl.ANY)] + [whole()] * peers,
        out_specs=[whole()] * 2,
        out_shape=[jax.ShapeDtypeStruct(shape, F32), jax.ShapeDtypeStruct(shape, BF16)],
        scratch_shapes=[
            pltpu.VMEM((peers, 2 * half, lanes), BF16),
            pltpu.VMEM((peers, shard, lanes), BF16),
            pltpu.VMEM((peers, shard, lanes), BF16),
            pltpu.SemaphoreType.DMA((peers, 3)),
        ],
        compiler_params=limits(16),
        name="last_grads",
    )(place, *[pltpu.with_memory_space_constraint(v, pltpu.HBM) for v in (wide, other)], *late)


def early_out(own_0, own_1, got_1, core):
    count, shard, half = own_0.shape

    def body(core_ref, own_0_ref, own_1_ref, got_1_ref, *outs):
        @pl.when(core_ref[0] == 0)
        def _():
            for i in range(count):
                outs[i][:, :half] = own_0_ref[i]

        @pl.when(core_ref[0] != 0)
        def _():
            for i in range(count):
                outs[i][:, :half] = got_1_ref[i].astype(F32)
                outs[i][:, half:] = own_1_ref[i]

    shape = jax.ShapeDtypeStruct((shard, half * CORES), F32)
    return pl.pallas_call(
        body,
        in_specs=[whole(pltpu.SMEM)] + [whole()] * 3,
        out_specs=[whole()] * count,
        out_shape=[shape] * count,
        compiler_params=limits(8),
        name="early_out",
    )(core, own_0, own_1, got_1)


def late_out(outs, got_0, core):
    count, shard, half = got_0.shape

    def body(core_ref, got_ref, *refs):
        wide_ref, sems = refs[-2:]
        targets = refs[count : 2 * count]

        @pl.when(core_ref[0] == 0)
        def _():
            copies = []
            for i in range(count):
                wide_ref[i] = got_ref[i].astype(F32)
                copy = pltpu.make_async_copy(
                    wide_ref.at[i], targets[i].at[:, half:], sems.at[i]
                )
                copy.start()
                copies.append(copy)
            for copy in copies:
                copy.wait()

    return pl.pallas_call(
        body,
        in_specs=[whole(pltpu.SMEM), whole()] + [whole(pl.ANY)] * count,
        out_specs=[whole(pl.ANY)] * count,
        out_shape=[jax.ShapeDtypeStruct(o.shape, o.dtype) for o in outs],
        scratch_shapes=[
            pltpu.VMEM((count, shard, half), F32),
            pltpu.SemaphoreType.DMA((count,)),
        ],
        input_output_aliases={2 + i: i for i in range(count)},
        compiler_params=limits(8),
        name="late_out",
    )(core, got_0, *outs)


def crossing(partial, residual, source, core, x, core_id, x_id):
    width = partial.shape[1] // XS
    split = partial.shape[0] // CORES
    own = columns_at(partial, x, width)
    pieces = fanned(lambda k: columns_at(partial, (x + k) % XS, width), "x", lambda k: k)

    total = own.astype(F32)
    for piece in pieces:
        total = total + piece.astype(F32)
    summed = lax.optimization_barrier(total.astype(BF16))
    halves = [summed[:split], summed[split:]]
    received = one_way(halves[1 - source], source)
    mine = jnp.where(core == source, halves[source], received)
    pieces = fanned(lambda k: mine, "zh", lambda k: k)
    total = mine.astype(F32)
    for piece in pieces:
        total = total + piece.astype(F32)
    out = (residual.astype(F32) + total).astype(BF16)
    blocks = [out] + fanned(lambda k: out, "x", lambda k: XS - k)
    gathered = assemble(blocks, x_id)
    other = shifted(gathered, "segment", 1)
    return merge(gathered, other, core_id)


def local(tokens, w_gate, w_up, w_down, cotangent):
    return step(tokens, w_gate[0], w_up[0], w_down[0], cotangent)


def step(tokens, gate_w, up_w, down_w, cotangent):
    core = lax.axis_index("segment")
    x = lax.axis_index("x")
    core_id = core.astype(jnp.int32)[None]
    x_id = x.astype(jnp.int32)[None]
    place = jnp.stack([core, lax.axis_index(DP)]).astype(jnp.int32)
    rows = tokens.shape[0]
    features, hidden = gate_w.shape
    half = hidden // CORES

    lent = one_way(down_w[half:], 0)
    down_half = lax.optimization_barrier(jnp.where(core == 0, down_w[:half], lent))
    own = spread(tokens.T, cotangent.T, core_id)
    gathered = exchanged(own, TENSOR)
    entered = gathered.reshape(features, rows)

    gate_a = dot_tn(entered, gate_w).astype(BF16)
    up_a = dot_tn(entered, up_w).astype(BF16)
    hidden_a = hidden_of(gate_a, up_a)
    partial_a = dot_nn(hidden_a, down_w).astype(BF16)
    block = lax.dynamic_slice_in_dim(entered, x * (features // XS), features // XS, 0).T
    first, second = block[: rows // CORES], block[rows // CORES :]
    other = shifted(jnp.where(core == 0, second, first), "segment", 1)
    residual_1 = jnp.where(core == 0, first, other)
    residual_2 = jnp.where(core == 0, other, second)
    middle = crossing(partial_a, residual_1, 0, core, x, core_id, x_id)

    d_hidden_a = lax.dot_general(
        entered, down_w, (((0,), (1,)), ((), ())), preferred_element_type=F32
    ).astype(BF16)
    d_hidden_a = lax.optimization_barrier(d_hidden_a)
    outgoing = picked([[(gate_a, 1), (up_a, 1)], [(d_hidden_a, 0)]], core_id)
    given = shifted(outgoing, "segment", 1)
    load = packed(
        [(gate_a, 0, 0), (up_a, 0, 1), (d_hidden_a, 1, 0)], given, entered, core_id
    )
    wide = exchanged(load, DP)

    wide_a = wide
    entered_other = shifted(wide[:, 3 * half :], "segment", 1)

    gate_b = dot_nn(middle, gate_w).astype(BF16)
    up_b = dot_nn(middle, up_w).astype(BF16)
    d_gate_b, d_up_b = gate_grads(d_hidden_a.astype(F32), gate_b, up_b)
    partial_b = (dot_nt(d_gate_b, gate_w) + dot_nt(d_up_b, up_w)).astype(BF16)
    upstream = crossing(partial_b, residual_2, 1, core, x, core_id, x_id)

    picks = [(gate_b, 0), (up_b, 0)]
    outgoing = picked([picks, picks], core_id)
    given = one_way(outgoing, 1)
    load = packed([(gate_b, 1, 0), (up_b, 1, 1)], given, (middle,), core_id, True)
    load, wide_a = lax.optimization_barrier((load, wide_a))
    wide_b = exchanged(load, DP)

    d_hidden_b = dot_nt(upstream, down_half).astype(BF16)
    late = list(packed_late(d_hidden_b, upstream, place))
    for k in range(1, PEERS):
        late[k] = shifted(late[k], DP, k)

    middle_other = shifted(wide_b[:, 2 * half :], "segment", 1)
    own_1, low_1 = first_grads(wide_b, wide_a, entered_other, middle_other, core_id)
    got_1 = one_way(low_1, 0)
    own_0, low_0 = last_grads(wide_a, entered_other, late, place)
    got_0 = one_way(low_0, 1)
    outs = early_out(own_0, own_1, got_1, core_id)
    grad_gate, grad_up, grad_down = late_out(outs, got_0, core_id)
    return (grad_gate[None], grad_up[None], grad_down.T[None])


def solution(mesh):
    fine = Mesh(
        mesh.devices.reshape(CORES, XS, ZH, ZL, YS), ("segment", "x", "zh", "zl", "y")
    )
    in_specs = (
        P(DP, TENSOR),
        P("segment", None, TENSOR),
        P("segment", None, TENSOR),
        P("segment", TENSOR, None),
        P(DP, TENSOR),
    )
    out_specs = (
        P("segment", DP, TENSOR),
        P("segment", DP, TENSOR),
        P("segment", TENSOR, DP),
    )
    return jax.shard_map(local, mesh=fine, in_specs=in_specs, out_specs=out_specs, check_vma=False)
```

profile of v0, /device:TPU:1, one launch (start us, length us, event | category | flops | bytes accessed | tf_op | source)
XLA Modules:
  0.0 178.3 jit_solution(13239539741097607910)
XLA Ops:
  1.6 26.2 %all_to_all.15 = bf16[16,96,128]{2,1,0:T(8,128)(2,1)S(1)} all-to-all(bf16[16,96,128]{2,1,0:T(8,128)(2,1)S(1)} %spread.1), channel_id=1, replica_groups=mesh['segment'=2,'x'=4,'zh'=4,'zl'=2,'y'=4] {'x','zh'}, dimensions={0} | all-to-all | bytes 786432 | tf_op jit(solution)/shard_map/all_to_all | solution.py:39
  30.5 2.3 %collective-permute-start.13 = (bf16[2,128,384]{2,1,0:T(8,128)(2,1)S(1)}, bf16[2,128,384]{2,1,0:T(8,128)(2,1)S(1)}, u32[]{:S(2)}, u32[]{:S(2)}) collective-permute-start(bf16[2,128,384]{2,1,0:T(8,128)(2,1)S(1)} %picked.3), channel_id=1, source_target_pairs={{0,128},{128,0},{1,129},{129,1},{2,130},{130,2},{3,131},{131,3},{4... | collective-permute-start | bytes 589832 | tf_op jit(solution)/shard_map/ppermute | solution.py:24
  35.9 4.8 %all-to-all-start.1 = ((bf16[8,1344,128]{2,1,0:T(8,128)(2,1)}), bf16[8,1344,128]{2,1,0:T(8,128)(2,1)}, u32[]{:S(2)}, u32[]{:S(2)}) async-start(bf16[8,1344,128]{2,1,0:T(8,128)(2,1)} %copy-done.1), calls=%async_computation.1 | async-start | bytes 5505024 | tf_op jit(solution)/shard_map/all_to_all | solution.py:39
  40.7 2.2 %convolution_convert_fusion = bf16[128,1536]{1,0:T(8,128)(2,1)S(1)} fusion(bf16[1,768,1536]{2,1,0:T(8,128)(2,1)} %param.8, bf16[128,768]{1,0:T(8,128)(2,1)S(1)} %fusion.21.refs_1_, bf16[128,768]{1,0:T(8,128)(2,1)S(1)} %fusion.15.refs_0_), kind=kOutput, calls=%fused_computation.2 | convolution fusion | flops 302972928 | bytes 3145728 | tf_op jit(solution)/shard_map/dot_general | solution.py:51
  43.6 1.8 collective-permute-start.2
  46.5 4.9 %collective-permute-done.1 = bf16[128,384]{1,0:T(8,128)(2,1)S(1)} collective-permute-done((bf16[128,384]{1,0:T(8,128)(2,1)}, bf16[128,384]{1,0:T(8,128)(2,1)S(1)}, u32[]{:S(2)}, u32[]{:S(2)}) %collective-permute-start.1) | collective-permute-done | bytes 98336 | tf_op jit(solution)/shard_map/ppermute | solution.py:24
  59.9 12.9 %collective-permute-done.5 = bf16[64,384]{1,0:T(8,128)(2,1)S(1)} collective-permute-done((bf16[64,384]{1,0:T(8,128)(2,1)S(1)}, bf16[64,384]{1,0:T(8,128)(2,1)S(1)}, u32[]{:S(2)}, u32[]{:S(2)}) %collective-permute-start.5) | collective-permute-done | bytes 49184 | tf_op jit(solution)/shard_map/ppermute | solution.py:24
  74.4 2.2 %collective-permute-start.8 = (bf16[64,384]{1,0:T(8,128)(2,1)S(1)}, bf16[64,384]{1,0:T(8,128)(2,1)S(1)}, u32[]{:S(2)}, u32[]{:S(2)}) collective-permute-start(bf16[64,384]{1,0:T(8,128)(2,1)S(1)} %add_convert_fusion.3.refs_0_), channel_id=1, source_target_pairs={{0,96},{32,0},{64,32},{96,64},{1,97},{33,1},{65,33},{97,65},{2,98}... | collective-permute-start | bytes 147464 | tf_op jit(solution)/shard_map/ppermute | solution.py:24
  78.2 3.0 %collective-permute-done.9.refs_2_ = bf16[64,384]{1,0:T(8,128)(2,1)S(1)} collective-permute-done((bf16[64,384]{1,0:T(8,128)(2,1)S(1)}, bf16[64,384]{1,0:T(8,128)(2,1)S(1)}, u32[]{:S(2)}, u32[]{:S(2)}) %collective-permute-start.9) | collective-permute-done | bytes 49184 | tf_op jit(solution)/shard_map/ppermute | solution.py:24
  81.2 3.8 %collective-permute-start.11 = (bf16[64,1536]{1,0:T(8,128)(2,1)S(1)}, bf16[64,1536]{1,0:T(8,128)(2,1)S(1)}, u32[]{:S(2)}, u32[]{:S(2)}) collective-permute-start(bf16[64,1536]{1,0:T(8,128)(2,1)S(1)} %assemble.2.own_ref), channel_id=1, source_target_pairs={{0,128},{128,0},{1,129},{129,1},{2,130},{130,2},{3,131},{131,3},{4... | collective-permute-start | bytes 589832 | tf_op jit(solution)/shard_map/ppermute | solution.py:24
  87.1 2.3 %collective-permute-start.12 = (bf16[2,128,384]{2,1,0:T(8,128)(2,1)S(1)}, bf16[2,128,384]{2,1,0:T(8,128)(2,1)S(1)}, u32[]{:S(2)}, u32[]{:S(2)}) collective-permute-start(bf16[2,128,384]{2,1,0:T(8,128)(2,1)S(1)} %picked.2), channel_id=1, source_target_pairs={{128,0},{129,1},{130,2},{131,3},{132,4},{133,5},{134,6},{135,7},{1... | collective-permute-start | bytes 589832 | tf_op jit(solution)/shard_map/ppermute | solution.py:35
  92.1 6.0 %all-to-all-start.2 = ((bf16[8,864,128]{2,1,0:T(8,128)(2,1)}), bf16[8,864,128]{2,1,0:T(8,128)(2,1)}, u32[]{:S(2)}, u32[]{:S(2)}) async-start(bf16[8,864,128]{2,1,0:T(8,128)(2,1)} %copy-done.2), calls=%async_computation.2 | async-start | bytes 3538944 | tf_op jit(solution)/shard_map/all_to_all | solution.py:39
  98.1 2.5 %slice_bitcast_fusion = bf16[384,1536]{1,0:T(8,128)(2,1)} fusion(bf16[1,768,1536]{2,1,0:T(8,128)(2,1)} %param.8), kind=kLoop, calls=%fused_computation.18 | loop fusion | bytes 2359296 | tf_op jit(solution)/shard_map/slice | solution.py:552
  106.6 3.5 %collective-permute-done.15 = bf16[128,384]{1,0:T(8,128)(2,1)S(1)} collective-permute-done((bf16[128,384]{1,0:T(8,128)(2,1)S(1)}, bf16[128,384]{1,0:T(8,128)(2,1)S(1)}, u32[]{:S(2)}, u32[]{:S(2)}) %collective-permute-start.15) | collective-permute-done | bytes 98336 | tf_op jit(solution)/shard_map/ppermute | solution.py:24
  110.8 5.1 %collective-permute-start.18 = (bf16[64,384]{1,0:T(8,128)(2,1)S(1)}, bf16[64,384]{1,0:T(8,128)(2,1)S(1)}, u32[]{:S(2)}, u32[]{:S(2)}) collective-permute-start(bf16[64,384]{1,0:T(8,128)(2,1)S(1)} %slice.54), channel_id=1, source_target_pairs={{128,0},{129,1},{130,2},{131,3},{132,4},{133,5},{134,6},{135,7},{1... | collective-permute-start | bytes 147464 | tf_op jit(solution)/shard_map/ppermute | solution.py:35
  117.9 4.2 %collective-permute-start.20 = (bf16[64,384]{1,0:T(8,128)(2,1)S(1)}, bf16[64,384]{1,0:T(8,128)(2,1)S(1)}, u32[]{:S(2)}, u32[]{:S(2)}) collective-permute-start(bf16[64,384]{1,0:T(8,128)(2,1)S(1)} %slice_select_fusion), channel_id=1, source_target_pairs={{0,16},{8,24},{16,0},{24,8},{1,17},{9,25},{17,1},{25,9},{2,18},{10... | collective-permute-start | bytes 147464 | tf_op jit(solution)/shard_map/ppermute | solution.py:24
  122.0 2.5 %collective-permute-start.21 = (bf16[64,384]{1,0:T(8,128)(2,1)S(1)}, bf16[64,384]{1,0:T(8,128)(2,1)S(1)}, u32[]{:S(2)}, u32[]{:S(2)}) collective-permute-start(bf16[64,384]{1,0:T(8,128)(2,1)S(1)} %slice_select_fusion), channel_id=1, source_target_pairs={{0,24},{8,0},{16,8},{24,16},{1,25},{9,1},{17,9},{25,17},{2,26},{10... | collective-permute-start | bytes 147464 | tf_op jit(solution)/shard_map/ppermute | solution.py:24
  124.8 4.3 %collective-permute-done.21 = bf16[64,384]{1,0:T(8,128)(2,1)S(1)} collective-permute-done((bf16[64,384]{1,0:T(8,128)(2,1)S(1)}, bf16[64,384]{1,0:T(8,128)(2,1)S(1)}, u32[]{:S(2)}, u32[]{:S(2)}) %collective-permute-start.21) | collective-permute-done | bytes 49184 | tf_op jit(solution)/shard_map/ppermute | solution.py:24
  129.2 2.1 %collective-permute-start.22 = (bf16[64,384]{1,0:T(8,128)(2,1)S(1)}, bf16[64,384]{1,0:T(8,128)(2,1)S(1)}, u32[]{:S(2)}, u32[]{:S(2)}) collective-permute-start(bf16[64,384]{1,0:T(8,128)(2,1)S(1)} %add_convert_fusion.2.refs_0_), channel_id=1, source_target_pairs={{0,96},{32,0},{64,32},{96,64},{1,97},{33,1},{65,33},{97,65},{2,98}... | collective-permute-start | bytes 147464 | tf_op jit(solution)/shard_map/ppermute | solution.py:24
  132.5 3.3 %collective-permute-done.23.refs_2_ = bf16[64,384]{1,0:T(8,128)(2,1)S(1)} collective-permute-done((bf16[64,384]{1,0:T(8,128)(2,1)S(1)}, bf16[64,384]{1,0:T(8,128)(2,1)S(1)}, u32[]{:S(2)}, u32[]{:S(2)}) %collective-permute-start.23) | collective-permute-done | bytes 49184 | tf_op jit(solution)/shard_map/ppermute | solution.py:24
  136.4 2.0 %collective-permute-start.25 = (bf16[64,1536]{1,0:T(8,128)(2,1)S(1)}, bf16[64,1536]{1,0:T(8,128)(2,1)S(1)}, u32[]{:S(2)}, u32[]{:S(2)}) collective-permute-start(bf16[64,1536]{1,0:T(8,128)(2,1)S(1)} %assemble.3.own_ref), channel_id=1, source_target_pairs={{0,128},{128,0},{1,129},{129,1},{2,130},{130,2},{3,131},{131,3},{4... | collective-permute-start | bytes 589832 | tf_op jit(solution)/shard_map/ppermute | solution.py:24
  138.4 2.9 %bitcast_select_fusion = bf16[384,1536]{1,0:T(8,128)(2,1)} fusion(bf16[384,1536]{1,0:T(8,128)(2,1)} %collective-permute-done.26, bf16[1,768,1536]{2,1,0:T(8,128)(2,1)} %param.8, pred[]{:T(512)S(6)} %eq.17), kind=kLoop, calls=%fused_computation.17 | loop fusion | flops 589824 | bytes 3538945 | tf_op jit(solution)/shard_map/jit(_where)/select_n | solution.py:553
  141.3 1.8 slice.52
  144.6 1.8 convolution_convert_fusion.1.grad_ref
  148.5 2.4 %collective-permute-start.28 = (bf16[576,128]{1,0:T(8,128)(2,1)S(1)}, bf16[576,128]{1,0:T(8,128)(2,1)S(1)}, u32[]{:S(2)}, u32[]{:S(2)}) collective-permute-start(bf16[576,128]{1,0:T(8,128)(2,1)S(1)} %get-tuple-element.26), channel_id=1, source_target_pairs={{0,2},{1,3},{2,4},{3,5},{4,6},{5,7},{6,0},{7,1},{8,10},{9,11},{10,... | collective-permute-start | bytes 442376 | tf_op jit(solution)/shard_map/ppermute | solution.py:24
  151.5 4.0 %collective-permute-done.27.refs_1_ = bf16[576,128]{1,0:T(8,128)(2,1)S(1)} collective-permute-done((bf16[576,128]{1,0:T(8,128)(2,1)S(1)}, bf16[576,128]{1,0:T(8,128)(2,1)S(1)}, u32[]{:S(2)}, u32[]{:S(2)}) %collective-permute-start.27) | collective-permute-done | bytes 147488 | tf_op jit(solution)/shard_map/ppermute | solution.py:24
  157.3 3.2 %collective-permute-start.31 = (bf16[576,128]{1,0:T(8,128)(2,1)S(1)}, bf16[576,128]{1,0:T(8,128)(2,1)S(1)}, u32[]{:S(2)}, u32[]{:S(2)}) collective-permute-start(bf16[576,128]{1,0:T(8,128)(2,1)S(1)} %get-tuple-element.29), channel_id=1, source_target_pairs={{0,5},{1,6},{2,7},{3,0},{4,1},{5,2},{6,3},{7,4},{8,13},{9,14},{10,... | collective-permute-start | bytes 442376 | tf_op jit(solution)/shard_map/ppermute | solution.py:24
  160.5 2.5 %collective-permute-start.33 = (bf16[576,128]{1,0:T(8,128)(2,1)S(1)}, bf16[576,128]{1,0:T(8,128)(2,1)S(1)}, u32[]{:S(2)}, u32[]{:S(2)}) collective-permute-start(bf16[576,128]{1,0:T(8,128)(2,1)S(1)} %get-tuple-element.31), channel_id=1, source_target_pairs={{0,7},{1,0},{2,1},{3,2},{4,3},{5,4},{6,5},{7,6},{8,15},{9,8},{10,9... | collective-permute-start | bytes 442376 | tf_op jit(solution)/shard_map/ppermute | solution.py:24
  163.0 3.2 %first_grads.1 = (f32[3,192,384]{2,1,0:T(8,128)S(1)}, bf16[3,192,384]{2,1,0:T(8,128)(2,1)S(1)}) custom-call(s32[1]{0:T(128)} %bitcast.core_ref, bf16[8,864,128]{2,1,0:T(8,128)(2,1)} %all-to-all-done.2.stored_ref, bf16[8,1344,128]{2,1,0:T(8,128)(2,1)} %all-to-all-done.1.wide_ref.entry_ref, bf16[8,192,128]{2,1,0:T(8,128)(2,1)} %copy-done.7, ...), custom_call_target="tpu_custom_call" | custom-call | tf_op jit(solution)/shard_map/first_grads/pallas_call | solution.py:329
  167.5 2.7 %collective-permute-done.32.refs_6_ = bf16[576,128]{1,0:T(8,128)(2,1)S(1)} collective-permute-done((bf16[576,128]{1,0:T(8,128)(2,1)S(1)}, bf16[576,128]{1,0:T(8,128)(2,1)S(1)}, u32[]{:S(2)}, u32[]{:S(2)}) %collective-permute-start.32) | collective-permute-done | bytes 147488 | tf_op jit(solution)/shard_map/ppermute | solution.py:24
  170.2 3.6 %last_grads.1 = (f32[3,192,384]{2,1,0:T(8,128)S(1)}, bf16[3,192,384]{2,1,0:T(8,128)(2,1)S(1)}) custom-call(s32[2]{0:T(128)S(1)} %pad_add_fusion.place_ref, bf16[8,1344,128]{2,1,0:T(8,128)(2,1)} %all-to-all-done.1.wide_ref.entry_ref, bf16[8,192,128]{2,1,0:T(8,128)(2,1)} %copy-done.7, bf16[576,128]{1,0:T(8,128)(2,1)S(1)} %get-tuple-element.24.refs_0_, ...), custom_call_target="tpu_custom_call" | custom-call | tf_op jit(solution)/shard_map/last_grads/pallas_call | solution.py:437
  173.8 2.9 %collective-permute-start.34 = (bf16[3,192,384]{2,1,0:T(8,128)(2,1)S(1)}, bf16[3,192,384]{2,1,0:T(8,128)(2,1)S(1)}, u32[]{:S(2)}, u32[]{:S(2)}) collective-permute-start(bf16[3,192,384]{2,1,0:T(8,128)(2,1)S(1)} %get-tuple-element.32), channel_id=1, source_target_pairs={{128,0},{129,1},{130,2},{131,3},{132,4},{133,5},{134,6},{135,7},{1... | collective-permute-start | bytes 1327112 | tf_op jit(solution)/shard_map/ppermute | solution.py:35
  (106 shorter events, 44.4 us)
Async XLA Ops:
  35.9 56.3 %all-to-all-start.1 = ((bf16[8,1344,128]{2,1,0:T(8,128)(2,1)}), bf16[8,1344,128]{2,1,0:T(8,128)(2,1)}, u32[]{:S(2)}, u32[]{:S(2)}) async-start(bf16[8,1344,128]{2,1,0:T(8,128)(2,1)} %copy-done.1), calls=%async_computation.1 | async-start | bytes 5505024 | tf_op jit(solution)/shard_map/all_to_all | solution.py:39
  43.6 7.7 %collective-permute-start.1 = (bf16[128,384]{1,0:T(8,128)(2,1)}, bf16[128,384]{1,0:T(8,128)(2,1)S(1)}, u32[]{:S(2)}, u32[]{:S(2)}) collective-permute-start(bf16[128,384]{1,0:T(8,128)(2,1)} %get-tuple-element.46), channel_id=1, source_target_pairs={{0,32},{32,64},{64,96},{96,0},{1,33},{33,65},{65,97},{97,1},{2,34}... | collective-permute-start | bytes 294920 | tf_op jit(solution)/shard_map/ppermute | solution.py:24
  43.6 7.7 %collective-permute-start.2 = (bf16[128,384]{1,0:T(8,128)(2,1)}, bf16[128,384]{1,0:T(8,128)(2,1)S(1)}, u32[]{:S(2)}, u32[]{:S(2)}) collective-permute-start(bf16[128,384]{1,0:T(8,128)(2,1)} %get-tuple-element.48), channel_id=1, source_target_pairs={{0,64},{32,96},{64,0},{96,32},{1,65},{33,97},{65,1},{97,33},{2,66}... | collective-permute-start | bytes 294920 | tf_op jit(solution)/shard_map/ppermute | solution.py:24
  45.4 6.0 %collective-permute-start.3 = (bf16[128,384]{1,0:T(8,128)(2,1)S(1)}, bf16[128,384]{1,0:T(8,128)(2,1)S(1)}, u32[]{:S(2)}, u32[]{:S(2)}) collective-permute-start(bf16[128,384]{1,0:T(8,128)(2,1)S(1)} %get-tuple-element.47), channel_id=1, source_target_pairs={{0,96},{32,0},{64,32},{96,64},{1,97},{33,1},{65,33},{97,65},{2,98}... | collective-permute-start | bytes 294920 | tf_op jit(solution)/shard_map/ppermute | solution.py:24
  53.7 6.2 %collective-permute-start = (bf16[64,384]{1,0:T(8,128)(2,1)S(1)}, bf16[64,384]{1,0:T(8,128)(2,1)S(1)}, u32[]{:S(2)}, u32[]{:S(2)}) collective-permute-start(bf16[64,384]{1,0:T(8,128)(2,1)S(1)} %broadcast_select_fusion), channel_id=1, source_target_pairs={{0,128},{128,0},{1,129},{129,1},{2,130},{130,2},{3,131},{131,3},{4... | collective-permute-start | bytes 147464 | tf_op jit(solution)/shard_map/ppermute | solution.py:24
  56.0 16.8 %collective-permute-start.5 = (bf16[64,384]{1,0:T(8,128)(2,1)S(1)}, bf16[64,384]{1,0:T(8,128)(2,1)S(1)}, u32[]{:S(2)}, u32[]{:S(2)}) collective-permute-start(bf16[64,384]{1,0:T(8,128)(2,1)S(1)} %slice_select_fusion.1), channel_id=1, source_target_pairs={{0,8},{8,16},{16,24},{24,0},{1,9},{9,17},{17,25},{25,1},{2,10},{10... | collective-permute-start | bytes 147464 | tf_op jit(solution)/shard_map/ppermute | solution.py:24
  56.5 17.3 %collective-permute-start.6 = (bf16[64,384]{1,0:T(8,128)(2,1)S(1)}, bf16[64,384]{1,0:T(8,128)(2,1)S(1)}, u32[]{:S(2)}, u32[]{:S(2)}) collective-permute-start(bf16[64,384]{1,0:T(8,128)(2,1)S(1)} %slice_select_fusion.1), channel_id=1, source_target_pairs={{0,16},{8,24},{16,0},{24,8},{1,17},{9,25},{17,1},{25,9},{2,18},{10... | collective-permute-start | bytes 147464 | tf_op jit(solution)/shard_map/ppermute | solution.py:24
  58.2 15.7 %collective-permute-start.7 = (bf16[64,384]{1,0:T(8,128)(2,1)S(1)}, bf16[64,384]{1,0:T(8,128)(2,1)S(1)}, u32[]{:S(2)}, u32[]{:S(2)}) collective-permute-start(bf16[64,384]{1,0:T(8,128)(2,1)S(1)} %slice_select_fusion.1), channel_id=1, source_target_pairs={{0,24},{8,0},{16,8},{24,16},{1,25},{9,1},{17,9},{25,17},{2,26},{10... | collective-permute-start | bytes 147464 | tf_op jit(solution)/shard_map/ppermute | solution.py:24
  76.7 4.5 %collective-permute-start.9 = (bf16[64,384]{1,0:T(8,128)(2,1)S(1)}, bf16[64,384]{1,0:T(8,128)(2,1)S(1)}, u32[]{:S(2)}, u32[]{:S(2)}) collective-permute-start(bf16[64,384]{1,0:T(8,128)(2,1)S(1)} %add_convert_fusion.3.refs_0_), channel_id=1, source_target_pairs={{0,64},{32,96},{64,0},{96,32},{1,65},{33,97},{65,1},{97,33},{2,66}... | collective-permute-start | bytes 147464 | tf_op jit(solution)/shard_map/ppermute | solution.py:24
  81.2 4.9 %collective-permute-start.11 = (bf16[64,1536]{1,0:T(8,128)(2,1)S(1)}, bf16[64,1536]{1,0:T(8,128)(2,1)S(1)}, u32[]{:S(2)}, u32[]{:S(2)}) collective-permute-start(bf16[64,1536]{1,0:T(8,128)(2,1)S(1)} %assemble.2.own_ref), channel_id=1, source_target_pairs={{0,128},{128,0},{1,129},{129,1},{2,130},{130,2},{3,131},{131,3},{4... | collective-permute-start | bytes 589832 | tf_op jit(solution)/shard_map/ppermute | solution.py:24
  92.1 50.9 %all-to-all-start.2 = ((bf16[8,864,128]{2,1,0:T(8,128)(2,1)}), bf16[8,864,128]{2,1,0:T(8,128)(2,1)}, u32[]{:S(2)}, u32[]{:S(2)}) async-start(bf16[8,864,128]{2,1,0:T(8,128)(2,1)} %copy-done.2), calls=%async_computation.2 | async-start | bytes 3538944 | tf_op jit(solution)/shard_map/all_to_all | solution.py:39
  100.6 37.8 %collective-permute-start.26 = (bf16[384,1536]{1,0:T(8,128)(2,1)}, bf16[384,1536]{1,0:T(8,128)(2,1)}, u32[]{:S(2)}, u32[]{:S(2)}) collective-permute-start(bf16[384,1536]{1,0:T(8,128)(2,1)} %slice_bitcast_fusion), channel_id=1, source_target_pairs={{0,128},{1,129},{2,130},{3,131},{4,132},{5,133},{6,134},{7,135},{8... | collective-permute-start | bytes 3538952 | tf_op jit(solution)/shard_map/ppermute | solution.py:35
  103.9 6.2 %collective-permute-start.15 = (bf16[128,384]{1,0:T(8,128)(2,1)S(1)}, bf16[128,384]{1,0:T(8,128)(2,1)S(1)}, u32[]{:S(2)}, u32[]{:S(2)}) collective-permute-start(bf16[128,384]{1,0:T(8,128)(2,1)S(1)} %get-tuple-element.43), channel_id=1, source_target_pairs={{0,32},{32,64},{64,96},{96,0},{1,33},{33,65},{65,97},{97,1},{2,34}... | collective-permute-start | bytes 294920 | tf_op jit(solution)/shard_map/ppermute | solution.py:24
  103.9 6.1 %collective-permute-start.16 = (bf16[128,384]{1,0:T(8,128)(2,1)S(1)}, bf16[128,384]{1,0:T(8,128)(2,1)S(1)}, u32[]{:S(2)}, u32[]{:S(2)}) collective-permute-start(bf16[128,384]{1,0:T(8,128)(2,1)S(1)} %get-tuple-element.45), channel_id=1, source_target_pairs={{0,64},{32,96},{64,0},{96,32},{1,65},{33,97},{65,1},{97,33},{2,66}... | collective-permute-start | bytes 294920 | tf_op jit(solution)/shard_map/ppermute | solution.py:24
  105.1 5.6 %collective-permute-start.17 = (bf16[128,384]{1,0:T(8,128)(2,1)S(1)}, bf16[128,384]{1,0:T(8,128)(2,1)S(1)}, u32[]{:S(2)}, u32[]{:S(2)}) collective-permute-start(bf16[128,384]{1,0:T(8,128)(2,1)S(1)} %get-tuple-element.44), channel_id=1, source_target_pairs={{0,96},{32,0},{64,32},{96,64},{1,97},{33,1},{65,33},{97,65},{2,98}... | collective-permute-start | bytes 294920 | tf_op jit(solution)/shard_map/ppermute | solution.py:24
  110.8 6.0 %collective-permute-start.18 = (bf16[64,384]{1,0:T(8,128)(2,1)S(1)}, bf16[64,384]{1,0:T(8,128)(2,1)S(1)}, u32[]{:S(2)}, u32[]{:S(2)}) collective-permute-start(bf16[64,384]{1,0:T(8,128)(2,1)S(1)} %slice.54), channel_id=1, source_target_pairs={{128,0},{129,1},{130,2},{131,3},{132,4},{133,5},{134,6},{135,7},{1... | collective-permute-start | bytes 147464 | tf_op jit(solution)/shard_map/ppermute | solution.py:35
  116.7 7.8 %collective-permute-start.19 = (bf16[64,384]{1,0:T(8,128)(2,1)S(1)}, bf16[64,384]{1,0:T(8,128)(2,1)S(1)}, u32[]{:S(2)}, u32[]{:S(2)}) collective-permute-start(bf16[64,384]{1,0:T(8,128)(2,1)S(1)} %slice_select_fusion), channel_id=1, source_target_pairs={{0,8},{8,16},{16,24},{24,0},{1,9},{9,17},{17,25},{25,1},{2,10},{10... | collective-permute-start | bytes 147464 | tf_op jit(solution)/shard_map/ppermute | solution.py:24
  117.9 7.0 %collective-permute-start.20 = (bf16[64,384]{1,0:T(8,128)(2,1)S(1)}, bf16[64,384]{1,0:T(8,128)(2,1)S(1)}, u32[]{:S(2)}, u32[]{:S(2)}) collective-permute-start(bf16[64,384]{1,0:T(8,128)(2,1)S(1)} %slice_select_fusion), channel_id=1, source_target_pairs={{0,16},{8,24},{16,0},{24,8},{1,17},{9,25},{17,1},{25,9},{2,18},{10... | collective-permute-start | bytes 147464 | tf_op jit(solution)/shard_map/ppermute | solution.py:24
  122.0 7.2 %collective-permute-start.21 = (bf16[64,384]{1,0:T(8,128)(2,1)S(1)}, bf16[64,384]{1,0:T(8,128)(2,1)S(1)}, u32[]{:S(2)}, u32[]{:S(2)}) collective-permute-start(bf16[64,384]{1,0:T(8,128)(2,1)S(1)} %slice_select_fusion), channel_id=1, source_target_pairs={{0,24},{8,0},{16,8},{24,16},{1,25},{9,1},{17,9},{25,17},{2,26},{10... | collective-permute-start | bytes 147464 | tf_op jit(solution)/shard_map/ppermute | solution.py:24
  131.4 4.5 %collective-permute-start.23 = (bf16[64,384]{1,0:T(8,128)(2,1)S(1)}, bf16[64,384]{1,0:T(8,128)(2,1)S(1)}, u32[]{:S(2)}, u32[]{:S(2)}) collective-permute-start(bf16[64,384]{1,0:T(8,128)(2,1)S(1)} %add_convert_fusion.2.refs_0_), channel_id=1, source_target_pairs={{0,64},{32,96},{64,0},{96,32},{1,65},{33,97},{65,1},{97,33},{2,66}... | collective-permute-start | bytes 147464 | tf_op jit(solution)/shard_map/ppermute | solution.py:24
  131.7 4.6 %collective-permute-start.24 = (bf16[64,384]{1,0:T(8,128)(2,1)S(1)}, bf16[64,384]{1,0:T(8,128)(2,1)S(1)}, u32[]{:S(2)}, u32[]{:S(2)}) collective-permute-start(bf16[64,384]{1,0:T(8,128)(2,1)S(1)} %add_convert_fusion.2.refs_0_), channel_id=1, source_target_pairs={{0,32},{32,64},{64,96},{96,0},{1,33},{33,65},{65,97},{97,1},{2,34}... | collective-permute-start | bytes 147464 | tf_op jit(solution)/shard_map/ppermute | solution.py:24
  136.4 4.9 %collective-permute-start.25 = (bf16[64,1536]{1,0:T(8,128)(2,1)S(1)}, bf16[64,1536]{1,0:T(8,128)(2,1)S(1)}, u32[]{:S(2)}, u32[]{:S(2)}) collective-permute-start(bf16[64,1536]{1,0:T(8,128)(2,1)S(1)} %assemble.3.own_ref), channel_id=1, source_target_pairs={{0,128},{128,0},{1,129},{129,1},{2,130},{130,2},{3,131},{131,3},{4... | collective-permute-start | bytes 589832 | tf_op jit(solution)/shard_map/ppermute | solution.py:24
  143.1 17.5 %collective-permute-start.14 = (bf16[8,192,128]{2,1,0:T(8,128)(2,1)}, bf16[8,192,128]{2,1,0:T(8,128)(2,1)S(1)}, u32[]{:S(2)}, u32[]{:S(2)}) collective-permute-start(bf16[8,192,128]{2,1,0:T(8,128)(2,1)} %slice.52), channel_id=1, source_target_pairs={{0,128},{128,0},{1,129},{129,1},{2,130},{130,2},{3,131},{131,3},{4... | collective-permute-start | bytes 1179656 | tf_op jit(solution)/shard_map/ppermute | solution.py:24
  144.0 16.5 %collective-permute-start.35 = (bf16[8,96,128]{2,1,0:T(8,128)(2,1)S(1)}, bf16[8,96,128]{2,1,0:T(8,128)(2,1)S(1)}, u32[]{:S(2)}, u32[]{:S(2)}) collective-permute-start(bf16[8,96,128]{2,1,0:T(8,128)(2,1)S(1)} %slice.55), channel_id=1, source_target_pairs={{0,128},{128,0},{1,129},{129,1},{2,130},{130,2},{3,131},{131,3},{4... | collective-permute-start | bytes 589832 | tf_op jit(solution)/shard_map/ppermute | solution.py:24
  147.2 8.4 %collective-permute-start.27 = (bf16[576,128]{1,0:T(8,128)(2,1)S(1)}, bf16[576,128]{1,0:T(8,128)(2,1)S(1)}, u32[]{:S(2)}, u32[]{:S(2)}) collective-permute-start(bf16[576,128]{1,0:T(8,128)(2,1)S(1)} %get-tuple-element.25), channel_id=1, source_target_pairs={{0,1},{1,2},{2,3},{3,4},{4,5},{5,6},{6,7},{7,0},{8,9},{9,10},{10,1... | collective-permute-start | bytes 442376 | tf_op jit(solution)/shard_map/ppermute | solution.py:24
  148.5 8.8 %collective-permute-start.28 = (bf16[576,128]{1,0:T(8,128)(2,1)S(1)}, bf16[576,128]{1,0:T(8,128)(2,1)S(1)}, u32[]{:S(2)}, u32[]{:S(2)}) collective-permute-start(bf16[576,128]{1,0:T(8,128)(2,1)S(1)} %get-tuple-element.26), channel_id=1, source_target_pairs={{0,2},{1,3},{2,4},{3,5},{4,6},{5,7},{6,0},{7,1},{8,10},{9,11},{10,... | collective-permute-start | bytes 442376 | tf_op jit(solution)/shard_map/ppermute | solution.py:24
  150.9 15.3 %collective-permute-start.29 = (bf16[576,128]{1,0:T(8,128)(2,1)S(1)}, bf16[576,128]{1,0:T(8,128)(2,1)S(1)}, u32[]{:S(2)}, u32[]{:S(2)}) collective-permute-start(bf16[576,128]{1,0:T(8,128)(2,1)S(1)} %get-tuple-element.27), channel_id=1, source_target_pairs={{0,3},{1,4},{2,5},{3,6},{4,7},{5,0},{6,1},{7,2},{8,11},{9,12},{10,... | collective-permute-start | bytes 442376 | tf_op jit(solution)/shard_map/ppermute | solution.py:24
  155.5 11.9 %collective-permute-start.30 = (bf16[576,128]{1,0:T(8,128)(2,1)S(1)}, bf16[576,128]{1,0:T(8,128)(2,1)S(1)}, u32[]{:S(2)}, u32[]{:S(2)}) collective-permute-start(bf16[576,128]{1,0:T(8,128)(2,1)S(1)} %get-tuple-element.28), channel_id=1, source_target_pairs={{0,4},{1,5},{2,6},{3,7},{4,0},{5,1},{6,2},{7,3},{8,12},{9,13},{10,... | collective-permute-start | bytes 442376 | tf_op jit(solution)/shard_map/ppermute | solution.py:24
  157.3 10.2 %collective-permute-start.31 = (bf16[576,128]{1,0:T(8,128)(2,1)S(1)}, bf16[576,128]{1,0:T(8,128)(2,1)S(1)}, u32[]{:S(2)}, u32[]{:S(2)}) collective-permute-start(bf16[576,128]{1,0:T(8,128)(2,1)S(1)} %get-tuple-element.29), channel_id=1, source_target_pairs={{0,5},{1,6},{2,7},{3,0},{4,1},{5,2},{6,3},{7,4},{8,13},{9,14},{10,... | collective-permute-start | bytes 442376 | tf_op jit(solution)/shard_map/ppermute | solution.py:24
  160.5 9.7 %collective-permute-start.32 = (bf16[576,128]{1,0:T(8,128)(2,1)S(1)}, bf16[576,128]{1,0:T(8,128)(2,1)S(1)}, u32[]{:S(2)}, u32[]{:S(2)}) collective-permute-start(bf16[576,128]{1,0:T(8,128)(2,1)S(1)} %get-tuple-element.30), channel_id=1, source_target_pairs={{0,6},{1,7},{2,0},{3,1},{4,2},{5,3},{6,4},{7,5},{8,14},{9,15},{10,... | collective-permute-start | bytes 442376 | tf_op jit(solution)/shard_map/ppermute | solution.py:24
  160.5 9.7 %collective-permute-start.33 = (bf16[576,128]{1,0:T(8,128)(2,1)S(1)}, bf16[576,128]{1,0:T(8,128)(2,1)S(1)}, u32[]{:S(2)}, u32[]{:S(2)}) collective-permute-start(bf16[576,128]{1,0:T(8,128)(2,1)S(1)} %get-tuple-element.31), channel_id=1, source_target_pairs={{0,7},{1,0},{2,1},{3,2},{4,3},{5,4},{6,5},{7,6},{8,15},{9,8},{10,9... | collective-permute-start | bytes 442376 | tf_op jit(solution)/shard_map/ppermute | solution.py:24
  166.2 10.5 %collective-permute-start.36 = (bf16[3,192,384]{2,1,0:T(8,128)(2,1)S(1)}, bf16[3,192,384]{2,1,0:T(8,128)(2,1)S(1)}, u32[]{:S(2)}, u32[]{:S(2)}) collective-permute-start(bf16[3,192,384]{2,1,0:T(8,128)(2,1)S(1)} %get-tuple-element.36), channel_id=1, source_target_pairs={{0,128},{1,129},{2,130},{3,131},{4,132},{5,133},{6,134},{7,135},{8... | collective-permute-start | bytes 1327112 | tf_op jit(solution)/shard_map/ppermute | solution.py:35
  (16 other events, 126.6 us)
where the time goes:
time: 180 us; the launch traced here: 178 us
  starting transfers between devices  69.4 us (39%)
  waiting for transfers between devices  48.3 us (27%)
  blocking collectives  26.2 us (15%)
  Pallas kernels  10.8 us (6%)
  local copies, waits for them, and re-layouts  9.66 us (5%)
  matrix products  8.62 us (5%)
  other arithmetic  4.07 us (2%)
    ppermute x31, waiting for transfers between devices, shifted(): lax.ppermute(value, axis, [(i, (i + distance) % size) for i in range(size)])  45.8 us
    ppermute x31, starting transfers between devices, shifted(): lax.ppermute(value, axis, [(i, (i + distance) % size) for i in range(size)])  44.4 us
    all_to_all x1, blocking collectives, exchanged(): return lax.all_to_all(value, axes, 0, 0, tiled=True)  26.2 us
    ppermute x6, starting transfers between devices, one_way(): return lax.ppermute(value, 'segment', [(source, 1 - source)])  14.3 us
    all_to_all x2, starting transfers between devices, exchanged(): return lax.all_to_all(value, axes, 0, 0, tiled=True)  10.8 us
    unnamed x19, local copies, waits for them, and re-layouts  3.62 us
  transfers between devices with their start and end apart: 39, of which 20 were waited for; matrix products, arithmetic and copies ran while one was open for 9% of the time, Pallas kernels for 5%

commit v1 on v0

--- a/solution.py
+++ b/solution.py
@@ -24,10 +24,14 @@
     return lax.ppermute(value, axis, [(i, (i + distance) % size) for i in range(size)])
 
 
-def fanned(value_of, axis, distance_of):
+def traded(value, axis, mask):
+    return lax.ppermute(value, axis, [(i, i ^ mask) for i in range(lax.axis_size(axis))])
+
+
+def fanned(value_of, axis):
     out = []
     for k in range(1, lax.axis_size(axis)):
-        out.append(shifted(value_of(k), axis, distance_of(k)))
+        out.append(traded(value_of(k), axis, k))
     return out
 
 
@@ -102,7 +106,7 @@
     def body(x_ref, *refs):
         out_ref = refs[-1]
         for k in range(XS):
-            start = pl.multiple_of(((x_ref[0] + k) % XS) * width, LANES)
+            start = pl.multiple_of((x_ref[0] ^ k) * width, LANES)
             out_ref[:, pl.ds(start, width)] = refs[k][...]
 
     return pl.pallas_call(
@@ -359,7 +363,7 @@
         for k in range(PEERS):
             for t in range(tiles):
                 outs[k][t * rows : (t + 1) * rows, :] = grad_ref[:, t * LANES : (t + 1) * LANES]
-            start = pl.multiple_of(((place_ref[1] + k) % PEERS) * shard, 64)
+            start = pl.multiple_of((place_ref[1] ^ k) * shard, 64)
             outs[k][tiles * rows :, :] = turned_ref[pl.ds(start, shard), :]
 
     shape = jax.ShapeDtypeStruct((tiles * rows + shard, rows), BF16)
@@ -385,7 +389,7 @@
         out_ref, low_ref, stored_ref, acts_ref, swapped_ref, sems = refs[peers:]
         copies = []
         for k in range(peers):
-            replica = (place_ref[1] + peers - k) % peers
+            replica = place_ref[1] ^ k
             moves = [
                 (wide_ref.at[replica, pl.ds(0, 2 * half)], stored_ref),
                 (wide_ref.at[replica, pl.ds(height - shard, shard)], acts_ref),
@@ -515,7 +519,7 @@
     width = partial.shape[1] // XS
     split = partial.shape[0] // CORES
     own = columns_at(partial, x, width)
-    pieces = fanned(lambda k: columns_at(partial, (x + k) % XS, width), "x", lambda k: k)
+    pieces = fanned(lambda k: columns_at(partial, x ^ k, width), "x")
 
     total = own.astype(F32)
     for piece in pieces:
@@ -524,12 +528,12 @@
     halves = [summed[:split], summed[split:]]
     received = one_way(halves[1 - source], source)
     mine = jnp.where(core == source, halves[source], received)
-    pieces = fanned(lambda k: mine, "zh", lambda k: k)
+    pieces = fanned(lambda k: mine, "zh")
     total = mine.astype(F32)
     for piece in pieces:
         total = total + piece.astype(F32)
     out = (residual.astype(F32) + total).astype(BF16)
-    blocks = [out] + fanned(lambda k: out, "x", lambda k: XS - k)
+    blocks = [out] + fanned(lambda k: out, "x")
     gathered = assemble(blocks, x_id)
     other = shifted(gathered, "segment", 1)
     return merge(gathered, other, core_id)
@@ -596,7 +600,7 @@
     d_hidden_b = dot_nt(upstream, down_half).astype(BF16)
     late = list(packed_late(d_hidden_b, upstream, place))
     for k in range(1, PEERS):
-        late[k] = shifted(late[k], DP, k)
+        late[k] = traded(late[k], DP, k)
 
     middle_other = shifted(wide_b[:, 2 * half :], "segment", 1)
     own_1, low_1 = first_grads(wide_b, wide_a, entered_other, middle_other, core_id)
@@ -624,4 +628,6 @@
         P("segment", DP, TENSOR),
         P("segment", TENSOR, DP),
     )
-    return jax.shard_map(local, mesh=fine, in_specs=in_specs, out_specs=out_specs, check_vma=False)
+    return jax.shard_map(
+        local, mesh=fine, in_specs=in_specs, out_specs=out_specs, check_vma=False
+    )

time: 180 us -> 179 us (level)
  starting transfers between devices: 69.4 us -> 75.1 us
  waiting for transfers between devices: 48.3 us -> 43.2 us
    ppermute x31 -> x6, waiting for transfers between devices: 45.8 us -> 2.15 us  [shifted(): lax.ppermute(value, axis, [(i, (i + distance) % size) for i in range(size)])]
    ppermute x0 -> x25, starting transfers between devices: none -> 39.3 us  [traded(): lax.ppermute(value, axis, [(i, i ^ mask) for i in range(lax.axis_size(axi...]
    ppermute x0 -> x25, waiting for transfers between devices: none -> 38.6 us  [traded(): lax.ppermute(value, axis, [(i, i ^ mask) for i in range(lax.axis_size(axi...]
    ppermute x31 -> x6, starting transfers between devices: 44.4 us -> 10.6 us  [shifted(): lax.ppermute(value, axis, [(i, (i + distance) % size) for i in range(size)])]
  transfers between devices with their start and end apart: 39 -> 39, of which waited for: 20 -> 22; matrix products, arithmetic and copies ran while one was open for 9% -> 9% of each run, Pallas kernels for 5% -> 5%
where the time goes in v1:
time: 179 us; the launch traced here: 178 us
  starting transfers between devices  75.1 us (42%)
  waiting for transfers between devices  43.2 us (24%)
  blocking collectives  26.2 us (15%)
  Pallas kernels  10.8 us (6%)
  local copies, waits for them, and re-layouts  8.91 us (5%)
  matrix products  8.63 us (5%)
  other arithmetic  4.06 us (2%)
    ppermute x25, starting transfers between devices, traded(): lax.ppermute(value, axis, [(i, i ^ mask) for i in range(lax.axis_size(axi...  39.3 us
    ppermute x25, waiting for transfers between devices, traded(): lax.ppermute(value, axis, [(i, i ^ mask) for i in range(lax.axis_size(axi...  38.6 us
    all_to_all x1, blocking collectives, exchanged(): return lax.all_to_all(value, axes, 0, 0, tiled=True)  26.2 us
    ppermute x6, starting transfers between devices, one_way(): return lax.ppermute(value, 'segment', [(source, 1 - source)])  15.7 us
    ppermute x6, starting transfers between devices, shifted(): lax.ppermute(value, axis, [(i, (i + distance) % size) for i in range(size)])  10.6 us
    all_to_all x2, starting transfers between devices, exchanged(): return lax.all_to_all(value, axes, 0, 0, tiled=True)  9.56 us
    unnamed x19, local copies, waits for them, and re-layouts  3.62 us
  transfers between devices with their start and end apart: 39, of which 22 were waited for; matrix products, arithmetic and copies ran while one was open for 9% of the time, Pallas kernels for 5%

profile of v1, /device:TPU:1, one launch (start us, length us, event | category | flops | bytes accessed | tf_op | source)
XLA Modules:
  0.0 178.2 jit_solution(9236010992199263557)
XLA Ops:
  1.6 26.2 %all_to_all.15 = bf16[16,96,128]{2,1,0:T(8,128)(2,1)S(1)} all-to-all(bf16[16,96,128]{2,1,0:T(8,128)(2,1)S(1)} %spread.1), channel_id=1, replica_groups=mesh['segment'=2,'x'=4,'zh'=4,'zl'=2,'y'=4] {'x','zh'}, dimensions={0} | all-to-all | bytes 786432 | tf_op jit(solution)/shard_map/all_to_all | solution.py:43
  30.5 2.3 %collective-permute-start.13 = (bf16[2,128,384]{2,1,0:T(8,128)(2,1)S(1)}, bf16[2,128,384]{2,1,0:T(8,128)(2,1)S(1)}, u32[]{:S(2)}, u32[]{:S(2)}) collective-permute-start(bf16[2,128,384]{2,1,0:T(8,128)(2,1)S(1)} %picked.3), channel_id=1, source_target_pairs={{0,128},{128,0},{1,129},{129,1},{2,130},{130,2},{3,131},{131,3},{4... | collective-permute-start | bytes 589832 | tf_op jit(solution)/shard_map/ppermute | solution.py:24
  35.9 4.8 %all-to-all-start.1 = ((bf16[8,1344,128]{2,1,0:T(8,128)(2,1)}), bf16[8,1344,128]{2,1,0:T(8,128)(2,1)}, u32[]{:S(2)}, u32[]{:S(2)}) async-start(bf16[8,1344,128]{2,1,0:T(8,128)(2,1)} %copy-done.1), calls=%async_computation.1 | async-start | bytes 5505024 | tf_op jit(solution)/shard_map/all_to_all | solution.py:43
  40.7 2.2 %convolution_convert_fusion = bf16[128,1536]{1,0:T(8,128)(2,1)S(1)} fusion(bf16[1,768,1536]{2,1,0:T(8,128)(2,1)} %param.8, bf16[128,768]{1,0:T(8,128)(2,1)S(1)} %fusion.21.refs_1_, bf16[128,768]{1,0:T(8,128)(2,1)S(1)} %fusion.15.refs_0_), kind=kOutput, calls=%fused_computation.2 | convolution fusion | flops 302972928 | bytes 3145728 | tf_op jit(solution)/shard_map/dot_general | solution.py:55
  45.4 2.1 %collective-permute-start.3 = (bf16[128,384]{1,0:T(8,128)(2,1)S(1)}, bf16[128,384]{1,0:T(8,128)(2,1)S(1)}, u32[]{:S(2)}, u32[]{:S(2)}) collective-permute-start(bf16[128,384]{1,0:T(8,128)(2,1)S(1)} %get-tuple-element.47), channel_id=1, source_target_pairs={{0,96},{32,64},{64,32},{96,0},{1,97},{33,65},{65,33},{97,1},{2,98}... | collective-permute-start | bytes 294920 | tf_op jit(solution)/shard_map/ppermute | solution.py:28
  47.7 2.6 %collective-permute-done.2 = bf16[128,384]{1,0:T(8,128)(2,1)S(1)} collective-permute-done((bf16[128,384]{1,0:T(8,128)(2,1)}, bf16[128,384]{1,0:T(8,128)(2,1)S(1)}, u32[]{:S(2)}, u32[]{:S(2)}) %collective-permute-start.2) | collective-permute-done | bytes 98336 | tf_op jit(solution)/shard_map/ppermute | solution.py:28
  50.3 2.3 %collective-permute-done.3 = bf16[128,384]{1,0:T(8,128)(2,1)S(1)} collective-permute-done((bf16[128,384]{1,0:T(8,128)(2,1)S(1)}, bf16[128,384]{1,0:T(8,128)(2,1)S(1)}, u32[]{:S(2)}, u32[]{:S(2)}) %collective-permute-start.3) | collective-permute-done | bytes 98336 | tf_op jit(solution)/shard_map/ppermute | solution.py:28
  57.2 2.2 %collective-permute-start.6 = (bf16[64,384]{1,0:T(8,128)(2,1)S(1)}, bf16[64,384]{1,0:T(8,128)(2,1)S(1)}, u32[]{:S(2)}, u32[]{:S(2)}) collective-permute-start(bf16[64,384]{1,0:T(8,128)(2,1)S(1)} %slice_select_fusion.1), channel_id=1, source_target_pairs={{0,16},{8,24},{16,0},{24,8},{1,17},{9,25},{17,1},{25,9},{2,18},{10... | collective-permute-start | bytes 147464 | tf_op jit(solution)/shard_map/ppermute | solution.py:28
  59.4 3.0 %collective-permute-start.7 = (bf16[64,384]{1,0:T(8,128)(2,1)S(1)}, bf16[64,384]{1,0:T(8,128)(2,1)S(1)}, u32[]{:S(2)}, u32[]{:S(2)}) collective-permute-start(bf16[64,384]{1,0:T(8,128)(2,1)S(1)} %slice_select_fusion.1), channel_id=1, source_target_pairs={{0,24},{8,16},{16,8},{24,0},{1,25},{9,17},{17,9},{25,1},{2,26},{10... | collective-permute-start | bytes 147464 | tf_op jit(solution)/shard_map/ppermute | solution.py:28
  62.4 10.2 %collective-permute-done.5 = bf16[64,384]{1,0:T(8,128)(2,1)S(1)} collective-permute-done((bf16[64,384]{1,0:T(8,128)(2,1)S(1)}, bf16[64,384]{1,0:T(8,128)(2,1)S(1)}, u32[]{:S(2)}, u32[]{:S(2)}) %collective-permute-start.5) | collective-permute-done | bytes 49184 | tf_op jit(solution)/shard_map/ppermute | solution.py:28
  76.4 2.6 %collective-permute-start.9 = (bf16[64,384]{1,0:T(8,128)(2,1)S(1)}, bf16[64,384]{1,0:T(8,128)(2,1)S(1)}, u32[]{:S(2)}, u32[]{:S(2)}) collective-permute-start(bf16[64,384]{1,0:T(8,128)(2,1)S(1)} %add_convert_fusion.3.refs_0_), channel_id=1, source_target_pairs={{0,64},{32,96},{64,0},{96,32},{1,65},{33,97},{65,1},{97,33},{2,66}... | collective-permute-start | bytes 147464 | tf_op jit(solution)/shard_map/ppermute | solution.py:28
  81.0 3.2 %collective-permute-start.11 = (bf16[64,1536]{1,0:T(8,128)(2,1)S(1)}, bf16[64,1536]{1,0:T(8,128)(2,1)S(1)}, u32[]{:S(2)}, u32[]{:S(2)}) collective-permute-start(bf16[64,1536]{1,0:T(8,128)(2,1)S(1)} %assemble.2.own_ref), channel_id=1, source_target_pairs={{0,128},{128,0},{1,129},{129,1},{2,130},{130,2},{3,131},{131,3},{4... | collective-permute-start | bytes 589832 | tf_op jit(solution)/shard_map/ppermute | solution.py:24
  86.3 2.3 %collective-permute-start.12 = (bf16[2,128,384]{2,1,0:T(8,128)(2,1)S(1)}, bf16[2,128,384]{2,1,0:T(8,128)(2,1)S(1)}, u32[]{:S(2)}, u32[]{:S(2)}) collective-permute-start(bf16[2,128,384]{2,1,0:T(8,128)(2,1)S(1)} %picked.2), channel_id=1, source_target_pairs={{128,0},{129,1},{130,2},{131,3},{132,4},{133,5},{134,6},{135,7},{1... | collective-permute-start | bytes 589832 | tf_op jit(solution)/shard_map/ppermute | solution.py:39
  91.3 4.8 %all-to-all-start.2 = ((bf16[8,864,128]{2,1,0:T(8,128)(2,1)}), bf16[8,864,128]{2,1,0:T(8,128)(2,1)}, u32[]{:S(2)}, u32[]{:S(2)}) async-start(bf16[8,864,128]{2,1,0:T(8,128)(2,1)} %copy-done.2), calls=%async_computation.2 | async-start | bytes 3538944 | tf_op jit(solution)/shard_map/all_to_all | solution.py:43
  96.1 2.5 %slice_bitcast_fusion = bf16[384,1536]{1,0:T(8,128)(2,1)} fusion(bf16[1,768,1536]{2,1,0:T(8,128)(2,1)} %param.8), kind=kLoop, calls=%fused_computation.18 | loop fusion | bytes 2359296 | tf_op jit(solution)/shard_map/slice | solution.py:556
  103.0 1.9 %collective-permute-start.16 = (bf16[128,384]{1,0:T(8,128)(2,1)S(1)}, bf16[128,384]{1,0:T(8,128)(2,1)S(1)}, u32[]{:S(2)}, u32[]{:S(2)}) collective-permute-start(bf16[128,384]{1,0:T(8,128)(2,1)S(1)} %get-tuple-element.45), channel_id=1, source_target_pairs={{0,64},{32,96},{64,0},{96,32},{1,65},{33,97},{65,1},{97,33},{2,66}... | collective-permute-start | bytes 294920 | tf_op jit(solution)/shard_map/ppermute | solution.py:28
  105.9 2.4 %collective-permute-done.16 = bf16[128,384]{1,0:T(8,128)(2,1)S(1)} collective-permute-done((bf16[128,384]{1,0:T(8,128)(2,1)S(1)}, bf16[128,384]{1,0:T(8,128)(2,1)S(1)}, u32[]{:S(2)}, u32[]{:S(2)}) %collective-permute-start.16) | collective-permute-done | bytes 98336 | tf_op jit(solution)/shard_map/ppermute | solution.py:28
  110.0 4.9 %collective-permute-start.18 = (bf16[64,384]{1,0:T(8,128)(2,1)S(1)}, bf16[64,384]{1,0:T(8,128)(2,1)S(1)}, u32[]{:S(2)}, u32[]{:S(2)}) collective-permute-start(bf16[64,384]{1,0:T(8,128)(2,1)S(1)} %slice.54), channel_id=1, source_target_pairs={{128,0},{129,1},{130,2},{131,3},{132,4},{133,5},{134,6},{135,7},{1... | collective-permute-start | bytes 147464 | tf_op jit(solution)/shard_map/ppermute | solution.py:39
  115.8 1.8 %collective-permute-start.19 = (bf16[64,384]{1,0:T(8,128)(2,1)S(1)}, bf16[64,384]{1,0:T(8,128)(2,1)S(1)}, u32[]{:S(2)}, u32[]{:S(2)}) collective-permute-start(bf16[64,384]{1,0:T(8,128)(2,1)S(1)} %slice_select_fusion), channel_id=1, source_target_pairs={{0,8},{8,0},{16,24},{24,16},{1,9},{9,1},{17,25},{25,17},{2,10},{10... | collective-permute-start | bytes 147464 | tf_op jit(solution)/shard_map/ppermute | solution.py:28
  117.7 4.2 %collective-permute-start.20 = (bf16[64,384]{1,0:T(8,128)(2,1)S(1)}, bf16[64,384]{1,0:T(8,128)(2,1)S(1)}, u32[]{:S(2)}, u32[]{:S(2)}) collective-permute-start(bf16[64,384]{1,0:T(8,128)(2,1)S(1)} %slice_select_fusion), channel_id=1, source_target_pairs={{0,16},{8,24},{16,0},{24,8},{1,17},{9,25},{17,1},{25,9},{2,18},{10... | collective-permute-start | bytes 147464 | tf_op jit(solution)/shard_map/ppermute | solution.py:28
  121.8 2.8 %collective-permute-done.20 = bf16[64,384]{1,0:T(8,128)(2,1)S(1)} collective-permute-done((bf16[64,384]{1,0:T(8,128)(2,1)S(1)}, bf16[64,384]{1,0:T(8,128)(2,1)S(1)}, u32[]{:S(2)}, u32[]{:S(2)}) %collective-permute-start.20) | collective-permute-done | bytes 49184 | tf_op jit(solution)/shard_map/ppermute | solution.py:28
  124.7 2.2 %collective-permute-done.21 = bf16[64,384]{1,0:T(8,128)(2,1)S(1)} collective-permute-done((bf16[64,384]{1,0:T(8,128)(2,1)S(1)}, bf16[64,384]{1,0:T(8,128)(2,1)S(1)}, u32[]{:S(2)}, u32[]{:S(2)}) %collective-permute-start.21) | collective-permute-done | bytes 49184 | tf_op jit(solution)/shard_map/ppermute | solution.py:28
  127.0 2.7 %collective-permute-start.23 = (bf16[64,384]{1,0:T(8,128)(2,1)S(1)}, bf16[64,384]{1,0:T(8,128)(2,1)S(1)}, u32[]{:S(2)}, u32[]{:S(2)}) collective-permute-start(bf16[64,384]{1,0:T(8,128)(2,1)S(1)} %add_convert_fusion.2.refs_0_), channel_id=1, source_target_pairs={{0,64},{32,96},{64,0},{96,32},{1,65},{33,97},{65,1},{97,33},{2,66}... | collective-permute-start | bytes 147464 | tf_op jit(solution)/shard_map/ppermute | solution.py:28
  131.7 2.8 %collective-permute-done.24.refs_3_ = bf16[64,384]{1,0:T(8,128)(2,1)S(1)} collective-permute-done((bf16[64,384]{1,0:T(8,128)(2,1)S(1)}, bf16[64,384]{1,0:T(8,128)(2,1)S(1)}, u32[]{:S(2)}, u32[]{:S(2)}) %collective-permute-start.24) | collective-permute-done | bytes 49184 | tf_op jit(solution)/shard_map/ppermute | solution.py:28
  134.6 3.2 %collective-permute-start.25 = (bf16[64,1536]{1,0:T(8,128)(2,1)S(1)}, bf16[64,1536]{1,0:T(8,128)(2,1)S(1)}, u32[]{:S(2)}, u32[]{:S(2)}) collective-permute-start(bf16[64,1536]{1,0:T(8,128)(2,1)S(1)} %assemble.3.own_ref), channel_id=1, source_target_pairs={{0,128},{128,0},{1,129},{129,1},{2,130},{130,2},{3,131},{131,3},{4... | collective-permute-start | bytes 589832 | tf_op jit(solution)/shard_map/ppermute | solution.py:24
  137.8 2.9 %bitcast_select_fusion = bf16[384,1536]{1,0:T(8,128)(2,1)} fusion(bf16[384,1536]{1,0:T(8,128)(2,1)} %collective-permute-done.26, bf16[1,768,1536]{2,1,0:T(8,128)(2,1)} %param.8, pred[]{:T(512)S(6)} %eq.4), kind=kLoop, calls=%fused_computation.17 | loop fusion | flops 589824 | bytes 3538945 | tf_op jit(solution)/shard_map/jit(_where)/select_n | solution.py:557
  147.4 2.4 %collective-permute-start.28 = (bf16[576,128]{1,0:T(8,128)(2,1)S(1)}, bf16[576,128]{1,0:T(8,128)(2,1)S(1)}, u32[]{:S(2)}, u32[]{:S(2)}) collective-permute-start(bf16[576,128]{1,0:T(8,128)(2,1)S(1)} %get-tuple-element.26), channel_id=1, source_target_pairs={{0,2},{1,3},{2,0},{3,1},{4,6},{5,7},{6,4},{7,5},{8,10},{9,11},{10,... | collective-permute-start | bytes 442376 | tf_op jit(solution)/shard_map/ppermute | solution.py:28
  153.1 3.9 %collective-permute-done.28.refs_2_ = bf16[576,128]{1,0:T(8,128)(2,1)S(1)} collective-permute-done((bf16[576,128]{1,0:T(8,128)(2,1)S(1)}, bf16[576,128]{1,0:T(8,128)(2,1)S(1)}, u32[]{:S(2)}, u32[]{:S(2)}) %collective-permute-start.28) | collective-permute-done | bytes 147488 | tf_op jit(solution)/shard_map/ppermute | solution.py:28
  159.1 4.1 %collective-permute-start.33 = (bf16[576,128]{1,0:T(8,128)(2,1)S(1)}, bf16[576,128]{1,0:T(8,128)(2,1)S(1)}, u32[]{:S(2)}, u32[]{:S(2)}) collective-permute-start(bf16[576,128]{1,0:T(8,128)(2,1)S(1)} %get-tuple-element.31), channel_id=1, source_target_pairs={{0,7},{1,6},{2,5},{3,4},{4,3},{5,2},{6,1},{7,0},{8,15},{9,14},{10,... | collective-permute-start | bytes 442376 | tf_op jit(solution)/shard_map/ppermute | solution.py:28
  163.2 3.2 %first_grads.1 = (f32[3,192,384]{2,1,0:T(8,128)S(1)}, bf16[3,192,384]{2,1,0:T(8,128)(2,1)S(1)}) custom-call(s32[1]{0:T(128)} %bitcast.core_ref, bf16[8,864,128]{2,1,0:T(8,128)(2,1)} %all-to-all-done.2.stored_ref, bf16[8,1344,128]{2,1,0:T(8,128)(2,1)} %all-to-all-done.1.wide_ref.entry_ref, bf16[8,192,128]{2,1,0:T(8,128)(2,1)} %copy-done.7, ...), custom_call_target="tpu_custom_call" | custom-call | tf_op jit(solution)/shard_map/first_grads/pallas_call | solution.py:333
  168.7 3.5 %last_grads.1 = (f32[3,192,384]{2,1,0:T(8,128)S(1)}, bf16[3,192,384]{2,1,0:T(8,128)(2,1)S(1)}) custom-call(s32[2]{0:T(128)S(1)} %pad_add_fusion.place_ref, bf16[8,1344,128]{2,1,0:T(8,128)(2,1)} %all-to-all-done.1.wide_ref.entry_ref, bf16[8,192,128]{2,1,0:T(8,128)(2,1)} %copy-done.7, bf16[576,128]{1,0:T(8,128)(2,1)S(1)} %get-tuple-element.24.refs_0_, ...), custom_call_target="tpu_custom_call" | custom-call | tf_op jit(solution)/shard_map/last_grads/pallas_call | solution.py:441
  172.3 4.3 %collective-permute-start.34 = (bf16[3,192,384]{2,1,0:T(8,128)(2,1)S(1)}, bf16[3,192,384]{2,1,0:T(8,128)(2,1)S(1)}, u32[]{:S(2)}, u32[]{:S(2)}) collective-permute-start(bf16[3,192,384]{2,1,0:T(8,128)(2,1)S(1)} %get-tuple-element.32), channel_id=1, source_target_pairs={{128,0},{129,1},{130,2},{131,3},{132,4},{133,5},{134,6},{135,7},{1... | collective-permute-start | bytes 1327112 | tf_op jit(solution)/shard_map/ppermute | solution.py:39
  (106 shorter events, 50.6 us)
Async XLA Ops:
  35.9 55.5 %all-to-all-start.1 = ((bf16[8,1344,128]{2,1,0:T(8,128)(2,1)}), bf16[8,1344,128]{2,1,0:T(8,128)(2,1)}, u32[]{:S(2)}, u32[]{:S(2)}) async-start(bf16[8,1344,128]{2,1,0:T(8,128)(2,1)} %copy-done.1), calls=%async_computation.1 | async-start | bytes 5505024 | tf_op jit(solution)/shard_map/all_to_all | solution.py:43
  43.6 6.6 %collective-permute-start.2 = (bf16[128,384]{1,0:T(8,128)(2,1)}, bf16[128,384]{1,0:T(8,128)(2,1)S(1)}, u32[]{:S(2)}, u32[]{:S(2)}) collective-permute-start(bf16[128,384]{1,0:T(8,128)(2,1)} %get-tuple-element.48), channel_id=1, source_target_pairs={{0,64},{32,96},{64,0},{96,32},{1,65},{33,97},{65,1},{97,33},{2,66}... | collective-permute-start | bytes 294920 | tf_op jit(solution)/shard_map/ppermute | solution.py:28
  45.4 7.2 %collective-permute-start.3 = (bf16[128,384]{1,0:T(8,128)(2,1)S(1)}, bf16[128,384]{1,0:T(8,128)(2,1)S(1)}, u32[]{:S(2)}, u32[]{:S(2)}) collective-permute-start(bf16[128,384]{1,0:T(8,128)(2,1)S(1)} %get-tuple-element.47), channel_id=1, source_target_pairs={{0,96},{32,64},{64,32},{96,0},{1,97},{33,65},{65,33},{97,1},{2,98}... | collective-permute-start | bytes 294920 | tf_op jit(solution)/shard_map/ppermute | solution.py:28
  54.9 7.6 %collective-permute-start = (bf16[64,384]{1,0:T(8,128)(2,1)S(1)}, bf16[64,384]{1,0:T(8,128)(2,1)S(1)}, u32[]{:S(2)}, u32[]{:S(2)}) collective-permute-start(bf16[64,384]{1,0:T(8,128)(2,1)S(1)} %broadcast_select_fusion), channel_id=1, source_target_pairs={{0,128},{128,0},{1,129},{129,1},{2,130},{130,2},{3,131},{131,3},{4... | collective-permute-start | bytes 147464 | tf_op jit(solution)/shard_map/ppermute | solution.py:24
  56.7 15.9 %collective-permute-start.5 = (bf16[64,384]{1,0:T(8,128)(2,1)S(1)}, bf16[64,384]{1,0:T(8,128)(2,1)S(1)}, u32[]{:S(2)}, u32[]{:S(2)}) collective-permute-start(bf16[64,384]{1,0:T(8,128)(2,1)S(1)} %slice_select_fusion.1), channel_id=1, source_target_pairs={{0,8},{8,0},{16,24},{24,16},{1,9},{9,1},{17,25},{25,17},{2,10},{10... | collective-permute-start | bytes 147464 | tf_op jit(solution)/shard_map/ppermute | solution.py:28
  57.2 16.6 %collective-permute-start.6 = (bf16[64,384]{1,0:T(8,128)(2,1)S(1)}, bf16[64,384]{1,0:T(8,128)(2,1)S(1)}, u32[]{:S(2)}, u32[]{:S(2)}) collective-permute-start(bf16[64,384]{1,0:T(8,128)(2,1)S(1)} %slice_select_fusion.1), channel_id=1, source_target_pairs={{0,16},{8,24},{16,0},{24,8},{1,17},{9,25},{17,1},{25,9},{2,18},{10... | collective-permute-start | bytes 147464 | tf_op jit(solution)/shard_map/ppermute | solution.py:28
  59.4 15.6 %collective-permute-start.7 = (bf16[64,384]{1,0:T(8,128)(2,1)S(1)}, bf16[64,384]{1,0:T(8,128)(2,1)S(1)}, u32[]{:S(2)}, u32[]{:S(2)}) collective-permute-start(bf16[64,384]{1,0:T(8,128)(2,1)S(1)} %slice_select_fusion.1), channel_id=1, source_target_pairs={{0,24},{8,16},{16,8},{24,0},{1,25},{9,17},{17,9},{25,1},{2,26},{10... | collective-permute-start | bytes 147464 | tf_op jit(solution)/shard_map/ppermute | solution.py:28
  75.0 4.2 %collective-permute-start.10 = (bf16[64,384]{1,0:T(8,128)(2,1)S(1)}, bf16[64,384]{1,0:T(8,128)(2,1)S(1)}, u32[]{:S(2)}, u32[]{:S(2)}) collective-permute-start(bf16[64,384]{1,0:T(8,128)(2,1)S(1)} %add_convert_fusion.3.refs_0_), channel_id=1, source_target_pairs={{0,96},{32,64},{64,32},{96,0},{1,97},{33,65},{65,33},{97,1},{2,98}... | collective-permute-start | bytes 147464 | tf_op jit(solution)/shard_map/ppermute | solution.py:28
  76.4 4.6 %collective-permute-start.9 = (bf16[64,384]{1,0:T(8,128)(2,1)S(1)}, bf16[64,384]{1,0:T(8,128)(2,1)S(1)}, u32[]{:S(2)}, u32[]{:S(2)}) collective-permute-start(bf16[64,384]{1,0:T(8,128)(2,1)S(1)} %add_convert_fusion.3.refs_0_), channel_id=1, source_target_pairs={{0,64},{32,96},{64,0},{96,32},{1,65},{33,97},{65,1},{97,33},{2,66}... | collective-permute-start | bytes 147464 | tf_op jit(solution)/shard_map/ppermute | solution.py:28
  81.0 4.2 %collective-permute-start.11 = (bf16[64,1536]{1,0:T(8,128)(2,1)S(1)}, bf16[64,1536]{1,0:T(8,128)(2,1)S(1)}, u32[]{:S(2)}, u32[]{:S(2)}) collective-permute-start(bf16[64,1536]{1,0:T(8,128)(2,1)S(1)} %assemble.2.own_ref), channel_id=1, source_target_pairs={{0,128},{128,0},{1,129},{129,1},{2,130},{130,2},{3,131},{131,3},{4... | collective-permute-start | bytes 589832 | tf_op jit(solution)/shard_map/ppermute | solution.py:24
  91.3 50.5 %all-to-all-start.2 = ((bf16[8,864,128]{2,1,0:T(8,128)(2,1)}), bf16[8,864,128]{2,1,0:T(8,128)(2,1)}, u32[]{:S(2)}, u32[]{:S(2)}) async-start(bf16[8,864,128]{2,1,0:T(8,128)(2,1)} %copy-done.2), calls=%async_computation.2 | async-start | bytes 3538944 | tf_op jit(solution)/shard_map/all_to_all | solution.py:43
  98.5 39.2 %collective-permute-start.26 = (bf16[384,1536]{1,0:T(8,128)(2,1)}, bf16[384,1536]{1,0:T(8,128)(2,1)}, u32[]{:S(2)}, u32[]{:S(2)}) collective-permute-start(bf16[384,1536]{1,0:T(8,128)(2,1)} %slice_bitcast_fusion), channel_id=1, source_target_pairs={{0,128},{1,129},{2,130},{3,131},{4,132},{5,133},{6,134},{7,135},{8... | collective-permute-start | bytes 3538952 | tf_op jit(solution)/shard_map/ppermute | solution.py:39
  103.0 5.4 %collective-permute-start.16 = (bf16[128,384]{1,0:T(8,128)(2,1)S(1)}, bf16[128,384]{1,0:T(8,128)(2,1)S(1)}, u32[]{:S(2)}, u32[]{:S(2)}) collective-permute-start(bf16[128,384]{1,0:T(8,128)(2,1)S(1)} %get-tuple-element.45), channel_id=1, source_target_pairs={{0,64},{32,96},{64,0},{96,32},{1,65},{33,97},{65,1},{97,33},{2,66}... | collective-permute-start | bytes 294920 | tf_op jit(solution)/shard_map/ppermute | solution.py:28
  104.9 5.1 %collective-permute-start.17 = (bf16[128,384]{1,0:T(8,128)(2,1)S(1)}, bf16[128,384]{1,0:T(8,128)(2,1)S(1)}, u32[]{:S(2)}, u32[]{:S(2)}) collective-permute-start(bf16[128,384]{1,0:T(8,128)(2,1)S(1)} %get-tuple-element.44), channel_id=1, source_target_pairs={{0,96},{32,64},{64,32},{96,0},{1,97},{33,65},{65,33},{97,1},{2,98}... | collective-permute-start | bytes 294920 | tf_op jit(solution)/shard_map/ppermute | solution.py:28
  110.0 5.8 %collective-permute-start.18 = (bf16[64,384]{1,0:T(8,128)(2,1)S(1)}, bf16[64,384]{1,0:T(8,128)(2,1)S(1)}, u32[]{:S(2)}, u32[]{:S(2)}) collective-permute-start(bf16[64,384]{1,0:T(8,128)(2,1)S(1)} %slice.54), channel_id=1, source_target_pairs={{128,0},{129,1},{130,2},{131,3},{132,4},{133,5},{134,6},{135,7},{1... | collective-permute-start | bytes 147464 | tf_op jit(solution)/shard_map/ppermute | solution.py:39
  115.8 6.0 %collective-permute-start.19 = (bf16[64,384]{1,0:T(8,128)(2,1)S(1)}, bf16[64,384]{1,0:T(8,128)(2,1)S(1)}, u32[]{:S(2)}, u32[]{:S(2)}) collective-permute-start(bf16[64,384]{1,0:T(8,128)(2,1)S(1)} %slice_select_fusion), channel_id=1, source_target_pairs={{0,8},{8,0},{16,24},{24,16},{1,9},{9,1},{17,25},{25,17},{2,10},{10... | collective-permute-start | bytes 147464 | tf_op jit(solution)/shard_map/ppermute | solution.py:28
  117.7 7.0 %collective-permute-start.20 = (bf16[64,384]{1,0:T(8,128)(2,1)S(1)}, bf16[64,384]{1,0:T(8,128)(2,1)S(1)}, u32[]{:S(2)}, u32[]{:S(2)}) collective-permute-start(bf16[64,384]{1,0:T(8,128)(2,1)S(1)} %slice_select_fusion), channel_id=1, source_target_pairs={{0,16},{8,24},{16,0},{24,8},{1,17},{9,25},{17,1},{25,9},{2,18},{10... | collective-permute-start | bytes 147464 | tf_op jit(solution)/shard_map/ppermute | solution.py:28
  121.8 5.1 %collective-permute-start.21 = (bf16[64,384]{1,0:T(8,128)(2,1)S(1)}, bf16[64,384]{1,0:T(8,128)(2,1)S(1)}, u32[]{:S(2)}, u32[]{:S(2)}) collective-permute-start(bf16[64,384]{1,0:T(8,128)(2,1)S(1)} %slice_select_fusion), channel_id=1, source_target_pairs={{0,24},{8,16},{16,8},{24,0},{1,25},{9,17},{17,9},{25,1},{2,26},{10... | collective-permute-start | bytes 147464 | tf_op jit(solution)/shard_map/ppermute | solution.py:28
  127.0 4.7 %collective-permute-start.23 = (bf16[64,384]{1,0:T(8,128)(2,1)S(1)}, bf16[64,384]{1,0:T(8,128)(2,1)S(1)}, u32[]{:S(2)}, u32[]{:S(2)}) collective-permute-start(bf16[64,384]{1,0:T(8,128)(2,1)S(1)} %add_convert_fusion.2.refs_0_), channel_id=1, source_target_pairs={{0,64},{32,96},{64,0},{96,32},{1,65},{33,97},{65,1},{97,33},{2,66}... | collective-permute-start | bytes 147464 | tf_op jit(solution)/shard_map/ppermute | solution.py:28
  129.7 4.8 %collective-permute-start.24 = (bf16[64,384]{1,0:T(8,128)(2,1)S(1)}, bf16[64,384]{1,0:T(8,128)(2,1)S(1)}, u32[]{:S(2)}, u32[]{:S(2)}) collective-permute-start(bf16[64,384]{1,0:T(8,128)(2,1)S(1)} %add_convert_fusion.2.refs_0_), channel_id=1, source_target_pairs={{0,96},{32,64},{64,32},{96,0},{1,97},{33,65},{65,33},{97,1},{2,98}... | collective-permute-start | bytes 147464 | tf_op jit(solution)/shard_map/ppermute | solution.py:28
  134.6 6.1 %collective-permute-start.25 = (bf16[64,1536]{1,0:T(8,128)(2,1)S(1)}, bf16[64,1536]{1,0:T(8,128)(2,1)S(1)}, u32[]{:S(2)}, u32[]{:S(2)}) collective-permute-start(bf16[64,1536]{1,0:T(8,128)(2,1)S(1)} %assemble.3.own_ref), channel_id=1, source_target_pairs={{0,128},{128,0},{1,129},{129,1},{2,130},{130,2},{3,131},{131,3},{4... | collective-permute-start | bytes 589832 | tf_op jit(solution)/shard_map/ppermute | solution.py:24
  141.7 16.7 %collective-permute-start.14 = (bf16[8,192,128]{2,1,0:T(8,128)(2,1)S(1)}, bf16[8,192,128]{2,1,0:T(8,128)(2,1)S(1)}, u32[]{:S(2)}, u32[]{:S(2)}) collective-permute-start(bf16[8,192,128]{2,1,0:T(8,128)(2,1)S(1)} %slice.52), channel_id=1, source_target_pairs={{0,128},{128,0},{1,129},{129,1},{2,130},{130,2},{3,131},{131,3},{4... | collective-permute-start | bytes 1179656 | tf_op jit(solution)/shard_map/ppermute | solution.py:24
  142.7 16.3 %collective-permute-start.35 = (bf16[8,96,128]{2,1,0:T(8,128)(2,1)S(1)}, bf16[8,96,128]{2,1,0:T(8,128)(2,1)S(1)}, u32[]{:S(2)}, u32[]{:S(2)}) collective-permute-start(bf16[8,96,128]{2,1,0:T(8,128)(2,1)S(1)} %slice.55), channel_id=1, source_target_pairs={{0,128},{128,0},{1,129},{129,1},{2,130},{130,2},{3,131},{131,3},{4... | collective-permute-start | bytes 589832 | tf_op jit(solution)/shard_map/ppermute | solution.py:24
  145.9 5.5 %collective-permute-start.27 = (bf16[576,128]{1,0:T(8,128)(2,1)S(1)}, bf16[576,128]{1,0:T(8,128)(2,1)S(1)}, u32[]{:S(2)}, u32[]{:S(2)}) collective-permute-start(bf16[576,128]{1,0:T(8,128)(2,1)S(1)} %get-tuple-element.25), channel_id=1, source_target_pairs={{0,1},{1,0},{2,3},{3,2},{4,5},{5,4},{6,7},{7,6},{8,9},{9,8},{10,11... | collective-permute-start | bytes 442376 | tf_op jit(solution)/shard_map/ppermute | solution.py:28
  147.4 9.5 %collective-permute-start.28 = (bf16[576,128]{1,0:T(8,128)(2,1)S(1)}, bf16[576,128]{1,0:T(8,128)(2,1)S(1)}, u32[]{:S(2)}, u32[]{:S(2)}) collective-permute-start(bf16[576,128]{1,0:T(8,128)(2,1)S(1)} %get-tuple-element.26), channel_id=1, source_target_pairs={{0,2},{1,3},{2,0},{3,1},{4,6},{5,7},{6,4},{7,5},{8,10},{9,11},{10,... | collective-permute-start | bytes 442376 | tf_op jit(solution)/shard_map/ppermute | solution.py:28
  149.8 16.5 %collective-permute-start.29 = (bf16[576,128]{1,0:T(8,128)(2,1)S(1)}, bf16[576,128]{1,0:T(8,128)(2,1)S(1)}, u32[]{:S(2)}, u32[]{:S(2)}) collective-permute-start(bf16[576,128]{1,0:T(8,128)(2,1)S(1)} %get-tuple-element.27), channel_id=1, source_target_pairs={{0,3},{1,2},{2,1},{3,0},{4,7},{5,6},{6,5},{7,4},{8,11},{9,10},{10,... | collective-permute-start | bytes 442376 | tf_op jit(solution)/shard_map/ppermute | solution.py:28
  151.4 16.3 %collective-permute-start.30 = (bf16[576,128]{1,0:T(8,128)(2,1)S(1)}, bf16[576,128]{1,0:T(8,128)(2,1)S(1)}, u32[]{:S(2)}, u32[]{:S(2)}) collective-permute-start(bf16[576,128]{1,0:T(8,128)(2,1)S(1)} %get-tuple-element.28), channel_id=1, source_target_pairs={{0,4},{1,5},{2,6},{3,7},{4,0},{5,1},{6,2},{7,3},{8,12},{9,13},{10,... | collective-permute-start | bytes 442376 | tf_op jit(solution)/shard_map/ppermute | solution.py:28
  157.0 10.7 %collective-permute-start.31 = (bf16[576,128]{1,0:T(8,128)(2,1)S(1)}, bf16[576,128]{1,0:T(8,128)(2,1)S(1)}, u32[]{:S(2)}, u32[]{:S(2)}) collective-permute-start(bf16[576,128]{1,0:T(8,128)(2,1)S(1)} %get-tuple-element.29), channel_id=1, source_target_pairs={{0,5},{1,4},{2,7},{3,6},{4,1},{5,0},{6,3},{7,2},{8,13},{9,12},{10,... | collective-permute-start | bytes 442376 | tf_op jit(solution)/shard_map/ppermute | solution.py:28
  158.4 9.3 %collective-permute-start.32 = (bf16[576,128]{1,0:T(8,128)(2,1)S(1)}, bf16[576,128]{1,0:T(8,128)(2,1)S(1)}, u32[]{:S(2)}, u32[]{:S(2)}) collective-permute-start(bf16[576,128]{1,0:T(8,128)(2,1)S(1)} %get-tuple-element.30), channel_id=1, source_target_pairs={{0,6},{1,7},{2,4},{3,5},{4,2},{5,3},{6,0},{7,1},{8,14},{9,15},{10,... | collective-permute-start | bytes 442376 | tf_op jit(solution)/shard_map/ppermute | solution.py:28
  159.1 9.7 %collective-permute-start.33 = (bf16[576,128]{1,0:T(8,128)(2,1)S(1)}, bf16[576,128]{1,0:T(8,128)(2,1)S(1)}, u32[]{:S(2)}, u32[]{:S(2)}) collective-permute-start(bf16[576,128]{1,0:T(8,128)(2,1)S(1)} %get-tuple-element.31), channel_id=1, source_target_pairs={{0,7},{1,6},{2,5},{3,4},{4,3},{5,2},{6,1},{7,0},{8,15},{9,14},{10,... | collective-permute-start | bytes 442376 | tf_op jit(solution)/shard_map/ppermute | solution.py:28
  166.3 10.3 %collective-permute-start.36 = (bf16[3,192,384]{2,1,0:T(8,128)(2,1)S(1)}, bf16[3,192,384]{2,1,0:T(8,128)(2,1)S(1)}, u32[]{:S(2)}, u32[]{:S(2)}) collective-permute-start(bf16[3,192,384]{2,1,0:T(8,128)(2,1)S(1)} %get-tuple-element.36), channel_id=1, source_target_pairs={{0,128},{1,129},{2,130},{3,131},{4,132},{5,133},{6,134},{7,135},{8... | collective-permute-start | bytes 1327112 | tf_op jit(solution)/shard_map/ppermute | solution.py:39
  172.3 5.7 %collective-permute-start.34 = (bf16[3,192,384]{2,1,0:T(8,128)(2,1)S(1)}, bf16[3,192,384]{2,1,0:T(8,128)(2,1)S(1)}, u32[]{:S(2)}, u32[]{:S(2)}) collective-permute-start(bf16[3,192,384]{2,1,0:T(8,128)(2,1)S(1)} %get-tuple-element.32), channel_id=1, source_target_pairs={{128,0},{129,1},{130,2},{131,3},{132,4},{133,5},{134,6},{135,7},{1... | collective-permute-start | bytes 1327112 | tf_op jit(solution)/shard_map/ppermute | solution.py:39
  (16 other events, 127.8 us)
